TPU v7x, 32 devices: a whole 2x2x4 slice. The times are simulated.
32 devices in a mesh: wide: 8 (over z, x), narrow: 4 (over y, core).
Axes of the slice: x: 2, y: 2, z: 4, core: 2. Of those that a mesh axis runs over, the one named last changes fastest.
Arguments:
- tokens: bfloat16 [16384, 768], P('wide'), may hold values from -6 to 6
- cotangent: bfloat16 [16384, 768], P(('wide', 'narrow')), may hold values from -6 to 6
- lengths: int32 [8, 8], P('wide'), may hold values from 1 to 576, 2048 in all within a row
- routes: int32 [16384, 2], P(('wide', 'narrow')), may hold values from 0 to 7, as said below
- capacity_slots: int32 [16384, 2], P(('wide', 'narrow')), may hold values from 0 to 135, as said below
- first_gain: float32 [768], replicated, may hold values from 0.5 to 1.5
- second_gain: float32 [768], replicated, may hold values from 0.5 to 1.5
- query_weight: bfloat16 [768, 768], P(None, 'narrow'), may hold values from -0.21875 to 0.21875
- key_weight: bfloat16 [768, 768], P(None, 'narrow'), may hold values from -0.21875 to 0.21875
- value_weight: bfloat16 [768, 768], P(None, 'narrow'), may hold values from -0.21875 to 0.21875
- out_weight: bfloat16 [768, 768], P('narrow'), may hold values from -2 to 2
- router_weight: bfloat16 [768, 8], replicated, may hold values from -0.15625 to 0.15625
- expert_in: bfloat16 [8, 768, 3072], P('wide', None, 'narrow'), may hold values from -0.21875 to 0.21875
- expert_out: bfloat16 [8, 3072, 768], P('wide', 'narrow'), may hold values from -0.75 to 0.75
Outputs:
- block_output: bfloat16 [16384, 768], P(('wide', 'narrow'))
- token_grad: float32 [16384, 768], P(('wide', 'narrow'))
- first_gain_grad: float32 [768], P('narrow')
- second_gain_grad: float32 [768], P('narrow')
- query_weight_grad: float32 [768, 768], P(None, 'narrow')
- key_weight_grad: float32 [768, 768], P(None, 'narrow')
- value_weight_grad: float32 [768, 768], P(None, 'narrow')
- out_weight_grad: float32 [768, 768], P('narrow')
- router_weight_grad: float32 [768, 8], P('narrow')
- expert_in_grad: float32 [8, 768, 3072], P('wide', None, 'narrow')
- expert_out_grad: float32 [8, 3072, 768], P('wide', 'narrow')
Inputs may be any that keep to these rules, and one draw needn't show every extreme that they name: `routes`: each row names two different experts. Within each device's block of 512 rows, the pairs that name one expert are ranked, all first choices before all second choices and in a fixed priority order among each; capacity_slots holds that rank, or 135 where the rank is 135 or more (a dropped pair). Kept pairs of one expert in one block have distinct slots.
All inputs are finite; a program needn't handle non-finite values.
Results may differ from a plain program's by a relative error of at most 0.019.
Values may be sent and summed in bfloat16 or wider, within the bound.
A program may use at most 192 MiB of HBM per device.

v0:
```python
import math

import jax
import jax.numpy as jnp
from jax import lax
from jax.sharding import PartitionSpec as P

HDIM = 64
TOK_DEV = 512
MAXLEN = 576
QBLK = 512


norm_eps = 1e-06
neg_large = -1e30


def matmul(left, right):
    return jnp.dot(left, right, preferred_element_type=jnp.float32)


def inner_rows(left, right):
    return lax.dot_general(
        left, right, (((0,), (0,)), ((), ())), preferred_element_type=jnp.float32
    )


def times_transposed(left, right):
    return lax.dot_general(
        left, right, (((1,), (1,)), ((), ())), preferred_element_type=jnp.float32
    )


def norm_rows(values):
    mean_row = jnp.mean(values, axis=-1, keepdims=True)
    centred = values - mean_row
    variance = jnp.mean(centred * centred, axis=-1, keepdims=True)
    root_inv = lax.rsqrt(variance + norm_eps)
    return (centred * root_inv, root_inv)


def norm_back(grad_scaled, normed, root_inv):
    first_mean = jnp.mean(grad_scaled, axis=-1, keepdims=True)
    second_mean = jnp.mean(grad_scaled * normed, axis=-1, keepdims=True)
    return root_inv * (grad_scaled - first_mean - normed * second_mean)


def gelu_parts(pre_act):
    normal_cdf = 0.5 * (1.0 + lax.erf(pre_act * 0.7071067811865476))
    density = jnp.exp(-0.5 * pre_act * pre_act) * 0.3989422804014327
    return (pre_act * normal_cdf, normal_cdf + pre_act * density)


def local(
    tokens,
    cotangent,
    lengths,
    routes,
    capacity_slots,
    first_gain,
    second_gain,
    query_weight,
    key_weight,
    value_weight,
    out_weight,
    router_weight,
    expert_in,
    expert_out,
):
    experts = lax.axis_size("wide")
    capacity = (42 * TOK_DEV + 20 * experts - 1) // (20 * experts)
    group_rows = tokens.shape[0]
    width = tokens.shape[1]
    window = QBLK + 2 * MAXLEN
    blocks = group_rows // QBLK
    local_heads = query_weight.shape[1] // HDIM
    score_scale = 1.0 / math.sqrt(HDIM)
    own_begin = lax.axis_index("narrow") * TOK_DEV
    whole_group = tokens.astype(jnp.float32)
    normed_one, root_one = norm_rows(whole_group)
    attn_in = (normed_one * first_gain).astype(jnp.bfloat16)
    queries = matmul(attn_in, query_weight).astype(jnp.bfloat16)
    keys_all = matmul(attn_in, key_weight).astype(jnp.bfloat16)
    values_all = matmul(attn_in, value_weight).astype(jnp.bfloat16)
    head_queries = queries.reshape(group_rows, local_heads, HDIM)
    head_keys = keys_all.reshape(group_rows, local_heads, HDIM)
    head_values = values_all.reshape(group_rows, local_heads, HDIM)
    image_ends = jnp.cumsum(lengths[0])
    positions = jnp.arange(group_rows, dtype=jnp.int32)
    segment = jnp.sum((positions[:, None] >= image_ends[None, :]).astype(jnp.int32), axis=1)

    def block_view(block_index):
        query_begin = block_index * QBLK
        key_begin = jnp.clip(query_begin - MAXLEN, 0, group_rows - window)
        query_block = lax.dynamic_slice_in_dim(head_queries, query_begin, QBLK, 0)
        key_block = lax.dynamic_slice_in_dim(head_keys, key_begin, window, 0)
        value_block = lax.dynamic_slice_in_dim(head_values, key_begin, window, 0)
        same_image = (
            lax.dynamic_slice_in_dim(segment, query_begin, QBLK, 0)[:, None]
            == lax.dynamic_slice_in_dim(segment, key_begin, window, 0)[None, :]
        )
        scores = (
            jnp.einsum("qhd,khd->hqk", query_block, key_block, preferred_element_type=jnp.float32)
            * score_scale
        )
        scores = jnp.where(same_image[None], scores, neg_large)
        return (query_begin, key_begin, query_block, key_block, value_block, scores)

    def attend_block(block_index):
        query_begin, key_begin, query_block, key_block, value_block, scores = block_view(
            block_index
        )
        row_top = jnp.max(scores, axis=2, keepdims=True)
        exponent = jnp.exp(scores - row_top)
        row_total = jnp.sum(exponent, axis=2, keepdims=True)
        weights = (exponent / row_total).astype(jnp.bfloat16)
        result = jnp.einsum(
            "hqk,khd->qhd", weights, value_block, preferred_element_type=jnp.float32
        )
        return (result.reshape(QBLK, local_heads * HDIM), (row_top + jnp.log(row_total))[:, :, 0])

    block_outputs, log_totals = lax.map(attend_block, jnp.arange(blocks, dtype=jnp.int32))
    attended = block_outputs.reshape(group_rows, local_heads * HDIM).astype(jnp.bfloat16)
    head_sum = lax.psum_scatter(
        matmul(attended, out_weight), "narrow", scatter_dimension=0, tiled=True
    )
    own_tokens = lax.dynamic_slice_in_dim(whole_group, own_begin, TOK_DEV, 0)
    own_normed = lax.dynamic_slice_in_dim(normed_one, own_begin, TOK_DEV, 0)
    own_root = lax.dynamic_slice_in_dim(root_one, own_begin, TOK_DEV, 0)
    hidden_one = own_tokens + head_sum
    normed_two, root_two = norm_rows(hidden_one)
    moe_in = (normed_two * second_gain).astype(jnp.bfloat16)
    logits = matmul(moe_in, router_weight)
    logit_top = jnp.max(logits, axis=1, keepdims=True)
    logit_exp = jnp.exp(logits - logit_top)
    router_probs = logit_exp / jnp.sum(logit_exp, axis=1, keepdims=True)
    expert_ids = jnp.arange(experts, dtype=jnp.int32)
    onehot = (routes[:, :, None] == expert_ids[None, None, :]).astype(jnp.float32)
    kept = (capacity_slots < capacity).astype(jnp.float32)
    gates = jnp.sum(onehot * router_probs[:, None, :], axis=2) * kept
    token_ids = jnp.broadcast_to(jnp.arange(TOK_DEV, dtype=jnp.int32)[:, None], routes.shape)
    slot_table = (
        jnp.full((experts, capacity + 1), TOK_DEV, jnp.int32)
        .at[routes, capacity_slots]
        .set(token_ids)[:, :capacity]
    )
    padded_in = jnp.concatenate([moe_in, jnp.zeros((1, width), jnp.bfloat16)], axis=0)
    arrived = lax.all_to_all(padded_in[slot_table], "wide", split_axis=0, concat_axis=0, tiled=True)
    slot_inputs = lax.all_gather(arrived[None], "narrow", axis=0, tiled=True).reshape(-1, width)
    pre_act = matmul(slot_inputs, expert_in[0])
    activated, gelu_slope = gelu_parts(pre_act)
    act_low = activated.astype(jnp.bfloat16)
    returned = lax.psum_scatter(
        matmul(act_low, expert_out[0]).astype(jnp.bfloat16),
        "narrow",
        scatter_dimension=0,
        tiled=True,
    ).reshape(arrived.shape)
    came_back = lax.all_to_all(returned, "wide", split_axis=0, concat_axis=0, tiled=True)
    pick_slots = jnp.minimum(capacity_slots, capacity - 1)
    pair_out = came_back[routes, pick_slots].astype(jnp.float32)
    mixed = hidden_one + jnp.sum(gates[:, :, None] * pair_out, axis=1)
    block_output = mixed.astype(jnp.bfloat16)
    grad_mixed = cotangent.astype(jnp.float32)
    grad_gates = jnp.sum(grad_mixed[:, None, :] * pair_out, axis=2) * kept
    grad_pairs = (gates[:, :, None] * grad_mixed[:, None, :]).astype(jnp.bfloat16)
    grad_slots = (
        jnp.zeros((experts, capacity + 1, width), jnp.bfloat16)
        .at[routes, capacity_slots]
        .set(grad_pairs)[:, :capacity]
    )
    grad_arrived = lax.all_to_all(grad_slots, "wide", split_axis=0, concat_axis=0, tiled=True)
    grad_flat = lax.all_gather(grad_arrived[None], "narrow", axis=0, tiled=True).reshape(-1, width)
    grad_act = times_transposed(grad_flat, expert_out[0])
    out_grad = inner_rows(act_low, grad_flat)[None]
    grad_pre = (grad_act * gelu_slope).astype(jnp.bfloat16)
    in_grad = inner_rows(slot_inputs, grad_pre)[None]
    grad_sent = lax.psum_scatter(
        times_transposed(grad_pre, expert_in[0]).astype(jnp.bfloat16),
        "narrow",
        scatter_dimension=0,
        tiled=True,
    ).reshape(arrived.shape)
    grad_home = lax.all_to_all(grad_sent, "wide", split_axis=0, concat_axis=0, tiled=True)
    pair_grads = grad_home[routes, pick_slots].astype(jnp.float32)
    grad_probs = jnp.sum(grad_gates[:, :, None] * onehot, axis=1)
    grad_logits = (
        router_probs * (grad_probs - jnp.sum(router_probs * grad_probs, axis=1, keepdims=True))
    ).astype(jnp.bfloat16)
    grad_moe_in = jnp.sum(pair_grads * kept[:, :, None], axis=1) + times_transposed(
        grad_logits, router_weight
    )
    router_grad = inner_rows(moe_in, grad_logits)
    second_part = jnp.sum(grad_moe_in * normed_two, axis=0)
    grad_hidden = grad_mixed + norm_back(grad_moe_in * second_gain, normed_two, root_two)
    grad_branch = lax.all_gather(grad_hidden.astype(jnp.bfloat16), "narrow", axis=0, tiled=True)
    out_weight_grad = inner_rows(attended, grad_branch)
    grad_attended = times_transposed(grad_branch, out_weight).astype(jnp.bfloat16)
    grad_heads = grad_attended.reshape(group_rows, local_heads, HDIM)

    def block_back(carry, block_index):
        grad_keys, grad_values = carry
        query_begin, key_begin, query_block, key_block, value_block, scores = block_view(
            block_index
        )
        probs = jnp.exp(scores - log_totals[block_index][:, :, None])
        grad_block = lax.dynamic_slice_in_dim(grad_heads, query_begin, QBLK, 0)
        grad_weights = jnp.einsum(
            "qhd,khd->hqk", grad_block, value_block, preferred_element_type=jnp.float32
        )
        inner_sum = jnp.sum(probs * grad_weights, axis=2, keepdims=True)
        grad_scores = (probs * (grad_weights - inner_sum)).astype(jnp.bfloat16)
        grad_query_block = (
            jnp.einsum("hqk,khd->qhd", grad_scores, key_block, preferred_element_type=jnp.float32)
            * score_scale
        )
        key_part = (
            jnp.einsum("hqk,qhd->khd", grad_scores, query_block, preferred_element_type=jnp.float32)
            * score_scale
        )
        value_part = jnp.einsum(
            "hqk,qhd->khd",
            probs.astype(jnp.bfloat16),
            grad_block,
            preferred_element_type=jnp.float32,
        )
        grad_keys = lax.dynamic_update_slice_in_dim(
            grad_keys,
            lax.dynamic_slice_in_dim(grad_keys, key_begin, window, 0) + key_part,
            key_begin,
            0,
        )
        grad_values = lax.dynamic_update_slice_in_dim(
            grad_values,
            lax.dynamic_slice_in_dim(grad_values, key_begin, window, 0) + value_part,
            key_begin,
            0,
        )
        return ((grad_keys, grad_values), grad_query_block)

    zero_heads = jnp.zeros((group_rows, local_heads, HDIM), jnp.float32)
    (grad_keys, grad_values), grad_query_blocks = lax.scan(
        block_back, (zero_heads, zero_heads), jnp.arange(blocks, dtype=jnp.int32)
    )
    grad_queries = grad_query_blocks.reshape(group_rows, local_heads * HDIM).astype(jnp.bfloat16)
    grad_keys_low = grad_keys.reshape(group_rows, local_heads * HDIM).astype(jnp.bfloat16)
    grad_values_low = grad_values.reshape(group_rows, local_heads * HDIM).astype(jnp.bfloat16)
    query_weight_grad = inner_rows(attn_in, grad_queries)
    key_weight_grad = inner_rows(attn_in, grad_keys_low)
    value_weight_grad = inner_rows(attn_in, grad_values_low)
    grad_attn_in = (
        times_transposed(grad_queries, query_weight)
        + times_transposed(grad_keys_low, key_weight)
        + times_transposed(grad_values_low, value_weight)
    )
    first_part = jnp.sum(grad_attn_in * normed_one, axis=0)
    grad_rows_att, router_share, first_share, second_share = (
        lax.psum_scatter(
            grad_attn_in.astype(jnp.bfloat16), "narrow", scatter_dimension=0, tiled=True
        ).astype(jnp.float32),
        lax.psum_scatter(
            router_grad.astype(jnp.bfloat16), "narrow", scatter_dimension=0, tiled=True
        ).astype(jnp.float32),
        lax.psum_scatter(
            first_part.astype(jnp.bfloat16), "narrow", scatter_dimension=0, tiled=True
        ).astype(jnp.float32),
        lax.psum_scatter(
            second_part.astype(jnp.bfloat16), "narrow", scatter_dimension=0, tiled=True
        ).astype(jnp.float32),
    )
    token_grad = grad_hidden + norm_back(grad_rows_att * first_gain, own_normed, own_root)
    summed = lax.psum(
        (
            query_weight_grad,
            key_weight_grad,
            value_weight_grad,
            out_weight_grad,
            router_share,
            first_share,
            second_share,
        ),
        "wide",
    )
    return (
        block_output,
        token_grad,
        summed[5],
        summed[6],
        summed[0],
        summed[1],
        summed[2],
        summed[3],
        summed[4],
        in_grad,
        out_grad,
    )


def solution(mesh):
    in_specs = (
        P("wide", None),
        P(("wide", "narrow"), None),
        P("wide", None),
        P(("wide", "narrow"), None),
        P(("wide", "narrow"), None),
        P(),
        P(),
        P(None, "narrow"),
        P(None, "narrow"),
        P(None, "narrow"),
        P("narrow", None),
        P(),
        P("wide", None, "narrow"),
        P("wide", "narrow", None),
    )
    out_specs = (
        P(("wide", "narrow"), None),
        P(("wide", "narrow"), None),
        P("narrow"),
        P("narrow"),
        P(None, "narrow"),
        P(None, "narrow"),
        P(None, "narrow"),
        P("narrow", None),
        P("narrow", None),
        P("wide", None, "narrow"),
        P("wide", "narrow", None),
    )
    return jax.shard_map(local, mesh=mesh, in_specs=in_specs, out_specs=out_specs, check_vma=False)
```

profile of v0, /device:TPU:0, one launch (start us, length us, event | category | flops | bytes accessed | tf_op | source)
XLA Modules:
  0.0 1127.4 jit_solution(10805821074884518010)
XLA Ops:
  18.7 53.4 %while.30 = (s32[]{:T(128)}, bf16[4,512,192]{1,2,0:T(8,128)(2,1)S(1)}, f32[4,3,512]{2,1,0:T(4,128)S(1)}, s32[4]{0:T(128)S(1)}, bf16[2048,3,64]{0,2,1:T(8,128)(2,...) while((s32[]{:T(128)}, ...), condition=%wide.region_7.8_spmd, body=%wide.region_4.7_spmd.sunk | while | flops 685832704 | bytes 36224776 | solution.py:122
  87.9 50.3 %reduce-scatter.8.cloned.1.call-done = f32[512,768]{1,0:T(8,128)} async-done(((f32[2048,768]{1,0:T(8,128)}), f32[512,768]{1,0:T(8,128)}) %reduce-scatter.8.cloned.1.call-update) | async-done | bytes 1572880 | tf_op jit(solution)/shard_map/reduce_scatter | solution.py:124
  149.7 45.1 %all_to_all.20 = bf16[8,135,768]{2,1,0:T(8,128)(2,1)S(1)} all-to-all(bf16[8,135,768]{2,1,0:T(8,128)(2,1)} %reshape.252), channel_id=1, replica_groups=mesh['wide'=8,'narrow'=4] {'wide'}, dimensions={0} | all-to-all | bytes 3317760 | tf_op jit(solution)/shard_map/all_to_all | solution.py:148
  196.4 46.0 %all-gather.8.cloned.1.call-done = bf16[32,135,768]{2,0,1:T(8,128)(2,1)} async-done(((bf16[8,135,768]{2,0,1:T(8,128)(2,1)}), bf16[32,135,768]{2,0,1:T(8,128)(2,1)}) %all-gather.8.cloned.1.call-update) | async-done | bytes 6635536 | tf_op jit(solution)/shard_map/all_gather | solution.py:149
  242.4 9.4 copy.141
  251.8 6.8 reshape.238
  258.6 11.4 %multiply_convert_fusion.1 = (bf16[4320,768]{1,0:T(8,128)(2,1)S(1)}, f32[4320,768]{1,0:T(8,128)}) fusion(bf16[4320,768]{1,0:T(8,128)(2,1)} %reshape.238, bf16[1,768,768]{2,1,0:T(8,128)(2,1)S(1)} %copy-done), kind=kOutput, calls=%fused_computation.57 | convolution fusion | flops 5112668160 | bytes 27721728 | tf_op jit(solution)/shard_map/dot_general | solution.py:19
  272.7 7.3 convolution_convert_fusion.1
  280.1 60.8 %reduce-scatter.10.cloned.1.call-done = bf16[1080,768]{1,0:T(8,128)(2,1)} async-done(((bf16[4320,768]{1,0:T(8,128)(2,1)}), bf16[1080,768]{1,0:T(8,128)(2,1)}) %reduce-scatter.10.cloned.1.call-update) | async-done | bytes 1658896 | tf_op jit(solution)/shard_map/reduce_scatter | solution.py:153
  343.9 5.6 all-to-all-start.1
  352.0 36.8 %all-to-all-done.1 = bf16[8,135,768]{2,1,0:T(8,128)(2,1)} async-done(((bf16[8,135,768]{2,1,0:T(8,128)(2,1)}), bf16[8,135,768]{2,1,0:T(8,128)(2,1)}, u32[]{:S(2)}, u32[]{:S(2)}) %all-to-all-start.1) | async-done | bytes 1658912 | tf_op jit(solution)/shard_map/all_to_all | solution.py:159
  390.6 13.4 %gather_fusion.1 = bf16[1024,768]{1,0:T(8,128)(2,1)} fusion(bf16[8,135,768]{2,0,1:T(8,128)(2,1)S(1)} %copy.143, s32[1024]{0:T(1024)S(1)} %reshape.259), kind=kCustom, calls=%fused_computation.1 | custom fusion | bytes 3153920 | tf_op jit(solution)/shard_map/gather | solution.py:161
  409.0 12.2 %multiply_reduce_fusion.3 = (f32[512,2]{1,0:T(8,128)S(1)}, f32[512,768]{1,0:T(8,128)}, bf16[512,2,768]{2,1,0:T(2,128)(2,1)}) fusion(f32[512,2,768]{2,1,0:T(2,128)} %reshape.289, f32[512,768]{1,0:T(8,128)S(1)} %copy-done.20, f32[512,2]{1,0:T(8,128)S(1)} %copy.134), kind=kLoop, calls=%fused_computation.67 | loop fusion | flops 4324352 | bytes 7872512 | tf_op jit(solution)/shard_map/reduce_sum | solution.py:165
  425.8 6.2 scatter_custom_fusion.1
  432.1 43.2 %all_to_all.21 = bf16[8,135,768]{2,1,0:T(8,128)(2,1)S(1)} all-to-all(bf16[8,135,768]{2,1,0:T(8,128)(2,1)S(1)} %bitcast.143), channel_id=1, replica_groups=mesh['wide'=8,'narrow'=4] {'wide'}, dimensions={0} | all-to-all | bytes 3317760 | tf_op jit(solution)/shard_map/all_to_all | solution.py:172
  477.0 45.9 %all-gather.10.cloned.1.call-done = bf16[32,135,768]{2,0,1:T(8,128)(2,1)} async-done(((bf16[8,135,768]{2,0,1:T(8,128)(2,1)}), bf16[32,135,768]{2,0,1:T(8,128)(2,1)}) %all-gather.10.cloned.1.call-update) | async-done | bytes 6635536 | tf_op jit(solution)/shard_map/all_gather | solution.py:173
  522.9 9.3 copy.145
  532.2 6.9 reshape.240
  539.1 11.5 %fusion.41 = bf16[4320,768]{1,0:T(8,128)(2,1)S(1)} fusion(f32[4320,768]{1,0:T(8,128)} %get-tuple-element.325, bf16[4320,768]{1,0:T(8,128)(2,1)} %reshape.240, bf16[1,768,768]{2,1,0:T(8,128)(2,1)S(1)} %copy-done.49), kind=kOutput, calls=%fused_computation.56 | convolution fusion | flops 5129256960 | bytes 27721728 | tf_op jit(solution)/shard_map/dot_general | solution.py:29
  553.4 7.4 convolution_convert_fusion
  560.8 60.8 %reduce-scatter.12.cloned.1.call-done = bf16[1080,768]{1,0:T(8,128)(2,1)} async-done(((bf16[4320,768]{1,0:T(8,128)(2,1)}), bf16[1080,768]{1,0:T(8,128)(2,1)}) %reduce-scatter.12.cloned.1.call-update) | async-done | bytes 1658896 | tf_op jit(solution)/shard_map/reduce_scatter | solution.py:178
  624.7 5.5 all-to-all-start.3
  631.0 38.4 %all-to-all-done.3 = bf16[8,135,768]{2,1,0:T(8,128)(2,1)} async-done(((bf16[8,135,768]{2,1,0:T(8,128)(2,1)}), bf16[8,135,768]{2,1,0:T(8,128)(2,1)}, u32[]{:S(2)}, u32[]{:S(2)}) %all-to-all-start.3) | async-done | bytes 1658912 | tf_op jit(solution)/shard_map/all_to_all | solution.py:184
  671.2 13.4 %gather_fusion.2 = bf16[1024,768]{1,0:T(8,128)(2,1)} fusion(bf16[8,135,768]{2,0,1:T(8,128)(2,1)S(1)} %copy.146, s32[1024]{0:T(1024)S(1)} %reshape.259), kind=kCustom, calls=%fused_computation.2 | custom fusion | bytes 3153920 | tf_op jit(solution)/shard_map/gather | solution.py:185
  689.5 16.2 %multiply_reduce_fusion.4 = f32[512,768]{1,0:T(8,128)S(1)} fusion(f32[512,2,768]{2,1,0:T(2,128)} %reshape.290, f32[512,2]{1,0:T(8,128)S(1)} %copy.147), kind=kLoop, calls=%fused_computation.68 | loop fusion | flops 1179648 | bytes 4722688 | tf_op jit(solution)/shard_map/reduce_sum | solution.py:190
  710.9 25.6 %all-gather.6.cloned.1.call-done = bf16[2048,768]{1,0:T(8,128)(2,1)} async-done(((bf16[512,768]{1,0:T(8,128)(2,1)}), bf16[2048,768]{1,0:T(8,128)(2,1)}) %all-gather.6.cloned.1.call-update) | async-done | bytes 3145744 | tf_op jit(solution)/shard_map/all_gather | solution.py:196
  743.1 206.8 %while.31 = (s32[]{:T(128)}, f32[2048,3,64]{0,2,1:T(8,128)}, f32[2048,3,64]{0,2,1:T(8,128)}, bf16[4,512,3,64]{1,3,2,0:T(8,128)(2,1)}, s32[4]{0:T(128)S(1)}, /*in...) while((s32[]{:T(128)}, f32[2048,3,64]{0,2,1:T(8,128)}, ...), condition=%wide.region_27.28_spmd, body=%wide.region_25.27_spmd.sunk | while | flops 1660688896 | bytes 159393760 | solution.py:242
  750.0 8.0 multiply_reduce_fusion.14
  757.9 10.0 multiply_convert_fusion.7
  773.4 7.5 dynamic_update_slice.45
  787.9 7.5 dynamic_update_slice.44
  802.1 8.0 multiply_reduce_fusion.14
  810.1 10.0 multiply_convert_fusion.7
  825.5 7.5 dynamic_update_slice.45
  840.1 7.5 dynamic_update_slice.44
  854.2 8.0 multiply_reduce_fusion.14
  862.2 10.0 multiply_convert_fusion.7
  877.6 7.1 dynamic_update_slice.45
  891.7 7.1 dynamic_update_slice.44
  905.4 8.0 multiply_reduce_fusion.14
  913.4 10.0 multiply_convert_fusion.7
  928.8 7.1 dynamic_update_slice.45
  942.9 7.1 dynamic_update_slice.44
  963.6 11.2 convolution_bitcast_fusion
  982.4 10.6 convolution_bitcast_fusion.1
  993.0 6.3 all-reduce.5
  999.4 39.2 %all-reduce.3 = (f32[192]{0:T(256)}, f32[192]{0:T(256)}, f32[192,8]{0,1:T(8,128)}) all-reduce(f32[192]{0:T(256)S(1)} %dynamic-slice_convert_fusion.1, f32[192]{0:T(256)S(1)} %dynamic-slice_convert_fusion, bf16[192,8]{0,1:T(8,128)(2,1)S(1)} %copy.151), channel_id=1, replica_groups=mesh['wide'=8,'narrow'=4] {'wide'}, use_global_device_ids=true, to_apply=%region_33.34 | all-reduce | flops 1920 | bytes 12288 | tf_op jit(solution)/shard_map/psum | solution.py:272
  1044.0 70.0 %all-reduce.8.cloned.1.call-done = (f32[768,192]{0,1:T(8,128)}, f32[768,192]{0,1:T(8,128)}, f32[768,192]{0,1:T(8,128)}, f32[192,768]{1,0:T(8,128)}) async-done(((f32[768,192]{0,1:T(8,128)}, f32[768,192]{0,1:T(8,128)}, f32[768,192]{0,1:T(8,128)}, f32[192,768]{1,0:T(8,128)}), (f32[768,192]{0,1:T(8,128)}, f32[768,192]{0,1:T(8,128)}, f32[768,192]{0,1:T(8,128)}, ...) | async-done | bytes 2359312 | tf_op jit(solution)/shard_map/psum | solution.py:272
  (322 shorter events, 235.4 us)
Async XLA Ops:
  7.2 251.4 %copy-start = (bf16[1,768,768]{2,1,0:T(8,128)(2,1)S(1)}, bf16[1,768,768]{2,1,0:T(8,128)(2,1)}, u32[]{:S(2)}) copy-start(bf16[1,768,768]{2,1,0:T(8,128)(2,1)} %param.30) | copy-start | bytes 3538948
  7.2 131.0 %reduce-scatter.8.cloned.1.call-start = ((), (), s32[]{:S(2)}) async-start(), calls=%async_computation.9 | async-start | bytes 7864320 | tf_op jit(solution)/shard_map/reduce_scatter | solution.py:124
  8.2 2.8 copy-start.4
  8.3 3.9 copy-start.43
  13.3 3.3 copy-start.10
  18.7 54.6 %copy-start.27 = (bf16[192,768]{1,0:T(8,128)(2,1)S(1)}, bf16[192,768]{1,0:T(8,128)(2,1)}, u32[]{:S(2)}) copy-start(bf16[192,768]{1,0:T(8,128)(2,1)} %param.28) | copy-start | bytes 884740
  72.1 4.8 copy-start.8
  77.0 165.4 %all-gather.8.cloned.1.call-start = ((), (), s32[]{:S(2)}) async-start(), calls=%async_computation.14 | async-start | bytes 8294400 | tf_op jit(solution)/shard_map/all_gather | solution.py:149
  77.5 5.1 copy-start.40
  77.5 5.1 copy-start.37
  77.5 5.1 copy-start.46
  77.6 5.2 copy-start.47
  87.9 53.6 %copy-start.42 = (f32[768]{0:T(1024)S(1)}, f32[768]{0:T(1024)}, u32[]{:S(2)}) copy-start(f32[768]{0:T(1024)} %param.24) | copy-start | bytes 9220
  141.7 209.7 %copy-start.14 = (bf16[512,768]{1,0:T(8,128)(2,1)}, bf16[512,768]{1,0:T(8,128)(2,1)S(1)}, u32[]{:S(2)}) copy-start(bf16[512,768]{1,0:T(8,128)(2,1)S(1)} %multiply_convert_fusion.4) | copy-start | bytes 2359300
  196.3 144.5 %reduce-scatter.10.cloned.1.call-start = ((), (), s32[]{:S(2)}) async-start(), calls=%async_computation.10 | async-start | bytes 8294400 | tf_op jit(solution)/shard_map/reduce_scatter | solution.py:153
  258.6 14.1 %copy-start.48 = (bf16[1,768,768]{2,1,0:T(8,128)(2,1)S(1)}, bf16[1,768,768]{2,1,0:T(8,128)(2,1)}, u32[]{:S(2)}) copy-start(bf16[1,768,768]{2,1,0:T(8,128)(2,1)} %param.31) | copy-start | bytes 3538948
  280.0 70.1 %copy-start.22 = (bf16[512,768]{1,0:T(8,128)(2,1)S(1)}, bf16[512,768]{1,0:T(8,128)(2,1)}, u32[]{:S(2)}) copy-start(bf16[512,768]{1,0:T(8,128)(2,1)} %param.19) | copy-start | bytes 2359300
  343.9 7.5 copy-start.41
  343.9 44.9 %all-to-all-start.1 = ((bf16[8,135,768]{2,1,0:T(8,128)(2,1)}), bf16[8,135,768]{2,1,0:T(8,128)(2,1)}, u32[]{:S(2)}, u32[]{:S(2)}) async-start(bf16[8,135,768]{2,1,0:T(8,128)(2,1)} %reshape.239), calls=%async_computation.3 | async-start | bytes 3342336 | tf_op jit(solution)/shard_map/all_to_all | solution.py:159
  349.6 173.3 %all-gather.10.cloned.1.call-start = ((), (), s32[]{:S(2)}) async-start(), calls=%async_computation.15 | async-start | bytes 8294400 | tf_op jit(solution)/shard_map/all_gather | solution.py:173
  404.0 5.0 copy-start.20
  476.8 144.8 %reduce-scatter.12.cloned.1.call-start = ((), (), s32[]{:S(2)}) async-start(), calls=%async_computation.11 | async-start | bytes 8294400 | tf_op jit(solution)/shard_map/reduce_scatter | solution.py:178
  532.2 6.9 copy-start.49
  624.7 44.7 %all-to-all-start.3 = ((bf16[8,135,768]{2,1,0:T(8,128)(2,1)}), bf16[8,135,768]{2,1,0:T(8,128)(2,1)}, u32[]{:S(2)}, u32[]{:S(2)}) async-start(bf16[8,135,768]{2,1,0:T(8,128)(2,1)} %reshape.241), calls=%async_computation.6 | async-start | bytes 3342336 | tf_op jit(solution)/shard_map/all_to_all | solution.py:184
  630.2 106.3 %all-gather.6.cloned.1.call-start = ((), (), s32[]{:S(2)}) async-start(), calls=%async_computation.12 | async-start | bytes 3932160 | tf_op jit(solution)/shard_map/all_gather | solution.py:196
  689.5 16.2 %copy-start.13 = (f32[512,768]{1,0:T(8,128)S(1)}, f32[512,768]{1,0:T(8,128)}, u32[]{:S(2)}) copy-start(f32[512,768]{1,0:T(8,128)} %copy-done.12) | copy-start | bytes 4718596
  707.3 29.2 %copy-start.28 = (bf16[192,768]{1,0:T(8,128)(2,1)S(1)}, bf16[192,768]{1,0:T(8,128)(2,1)}, u32[]{:S(2)}) copy-start(bf16[192,768]{1,0:T(8,128)(2,1)} %param.28) | copy-start | bytes 884740
  709.7 253.1 %reduce-scatter.16.cloned.1.call-start = ((), (), s32[]{:S(2)}) async-start(), calls=%async_computation.16 | async-start | bytes 245760
  710.8 327.8 %reduce-scatter.14.cloned.1.call-start = ((), (), s32[]{:S(2)}) async-start(), calls=%async_computation.13 | async-start | bytes 3932160 | tf_op jit(solution)/shard_map/reduce_scatter | solution.py:258
  749.9 8.0 copy-start.2
  767.9 12.9 %copy-start.24 = (bf16[4,512,3,64]{1,3,2,0:T(8,128)(2,1)S(1)}, bf16[4,512,3,64]{1,3,2,0:T(8,128)(2,1)}, u32[]{:S(2)}) copy-start(bf16[4,512,3,64]{1,3,2,0:T(8,128)(2,1)} %get-tuple-element.519) | copy-start | bytes 2359300 | tf_op jit(solution)/shard_map/while
  780.9 4.3 copy-start.3
  802.1 8.0 copy-start.2
  820.1 12.9 %copy-start.24 = (bf16[4,512,3,64]{1,3,2,0:T(8,128)(2,1)S(1)}, bf16[4,512,3,64]{1,3,2,0:T(8,128)(2,1)}, u32[]{:S(2)}) copy-start(bf16[4,512,3,64]{1,3,2,0:T(8,128)(2,1)} %get-tuple-element.519) | copy-start | bytes 2359300 | tf_op jit(solution)/shard_map/while
  833.0 4.3 copy-start.3
  854.2 8.0 copy-start.2
  872.2 12.5 %copy-start.24 = (bf16[4,512,3,64]{1,3,2,0:T(8,128)(2,1)S(1)}, bf16[4,512,3,64]{1,3,2,0:T(8,128)(2,1)}, u32[]{:S(2)}) copy-start(bf16[4,512,3,64]{1,3,2,0:T(8,128)(2,1)} %get-tuple-element.519) | copy-start | bytes 2359300 | tf_op jit(solution)/shard_map/while
  884.6 4.3 copy-start.3
  905.4 8.0 copy-start.2
  923.4 12.5 %copy-start.24 = (bf16[4,512,3,64]{1,3,2,0:T(8,128)(2,1)S(1)}, bf16[4,512,3,64]{1,3,2,0:T(8,128)(2,1)}, u32[]{:S(2)}) copy-start(bf16[4,512,3,64]{1,3,2,0:T(8,128)(2,1)} %get-tuple-element.519) | copy-start | bytes 2359300 | tf_op jit(solution)/shard_map/while
  935.8 4.3 copy-start.3
  960.9 153.1 %all-reduce.8.cloned.1.call-start = ((), (), s32[]{:S(2)}) async-start(), calls=%async_computation.17 | async-start | bytes 4718592 | tf_op jit(solution)/shard_map/psum | solution.py:272
  963.6 11.2 copy-start.11
  982.4 10.6 copy-start.45
  982.4 56.3 %copy-start.44 = (f32[768]{0:T(1024)S(1)}, f32[768]{0:T(1024)}, u32[]{:S(2)}) copy-start(f32[768]{0:T(1024)} %param.23) | copy-start | bytes 9220
  993.0 47.7 %copy-start.19 = (f32[512,768]{1,0:T(8,128)S(1)}, f32[512,768]{1,0:T(8,128)}, u32[]{:S(2)}) copy-start(f32[512,768]{1,0:T(8,128)} %get-tuple-element.312) | copy-start | bytes 4718596
  1040.7 79.9 %copy-start.1 = (bf16[1,768,768]{2,1,0:T(8,128)(2,1)S(1)}, bf16[1,768,768]{2,1,0:T(8,128)(2,1)}, u32[]{:S(2)}) copy-start(bf16[1,768,768]{2,1,0:T(8,128)(2,1)} %param.30) | copy-start | bytes 3538948
  1114.0 5.8 copy-start.26
  (28 other events, 53.4 us)
Sparse Core Ops, SparseCore 0:
  77.1 61.0 reduce-scatter.7
  196.4 45.9 all-gather.7
  280.2 60.6 reduce-scatter.9
  476.9 45.9 all-gather.9
  560.9 60.6 reduce-scatter.11
  709.8 26.6 all-gather.5
  739.7 19.7 reduce-scatter.15
  961.0 37.9 reduce-scatter.13
  1003.5 110.4 all-reduce.7
where the time goes:
time: 1140 us; the launch traced here: 1130 us
  waiting for transfers between devices  435 us (38%)
  matrix products  213 us (19%)
  local copies, waits for them, and re-layouts  195 us (17%)
  blocking collectives  134 us (12%)
  other arithmetic  108 us (9%)
  between operations  15.5 us (1%)
  loops' own time  13.6 us (1%)
  starting transfers between devices  12.8 us (1%)
    psum x1, waiting for transfers between devices, local(): lax.psum((query_weight_grad, key_weight_grad, value_weight_grad, out_weig...  70 us
    reduce_scatter x1, waiting for transfers between devices, local(): lax.psum_scatter(times_transposed(grad_pre, expert_in[0]).astype(jnp.bflo...  60.8 us
    reduce_scatter x1, waiting for transfers between devices, local(): lax.psum_scatter(matmul(act_low, expert_out[0]).astype(jnp.bfloat16), 'na...  60.8 us
    reduce_scatter x1, waiting for transfers between devices, local(): lax.psum_scatter(matmul(attended, out_weight), 'narrow', scatter_dimensio...  50.3 us
    all_gather x1, waiting for transfers between devices, local(): lax.all_gather(arrived[None], 'narrow', axis=0, tiled=True)  46 us
    all_gather x1, waiting for transfers between devices, local(): lax.all_gather(grad_arrived[None], 'narrow', axis=0, tiled=True)  45.9 us
    dot_general x8, matrix products, block_view(): jnp.einsum('qhd,khd->hqk', query_block, key_block, preferred_element_type...  45.8 us
    all_to_all x1, blocking collectives, local(): lax.all_to_all(padded_in[slot_table], 'wide', split_axis=0, concat_axis=0...  45.1 us
  transfers between devices with their start and end apart: 11, of which 9 were waited for; matrix products, arithmetic and copies ran while one was open for 23% of the time, Pallas kernels for 0%

commit v1 on v0

v1 whole, which is shorter than its diff:
```python
import functools
import math

import jax
import jax.numpy as jnp
from jax import lax
from jax.experimental import pallas as pl
from jax.experimental.pallas import tpu as pltpu
from jax.sharding import PartitionSpec as P

HDIM = 64
TILE = 256
BIG = 1e30
norm_eps = 1e-06
F32, BF16 = jnp.float32, jnp.bfloat16


def dot_nn(a, b):
    return lax.dot_general(a, b, (((1,), (0,)), ((), ())), preferred_element_type=F32)


def dot_nt(a, b):
    return lax.dot_general(a, b, (((1,), (1,)), ((), ())), preferred_element_type=F32)


def image_bounds(len_ref):
    ends = []
    total = jnp.int32(0)
    for image in range(len_ref.shape[1]):
        total = total + len_ref[0, image]
        ends.append(total)
    return [jnp.int32(0)] + ends[:-1], ends


def tile_range(starts, ends, tile):
    first, last = tile * TILE, tile * TILE + (TILE - 1)
    low, high = jnp.int32(0), jnp.int32(0)
    for begin, end in zip(starts, ends):
        low = jnp.where((begin <= first) & (first < end), begin, low)
        high = jnp.where((begin <= last) & (last < end), end, high)
    return low // TILE, (high + (TILE - 1)) // TILE


def head_mask(width, head, lanes):
    lane = lax.broadcasted_iota(jnp.int32, (1, lanes), 1)
    return ((lane >= head * HDIM) & (lane < (head + 1) * HDIM)) | (lane >= width)


def fwd_kernel(len_ref, tok_ref, gain_ref, wq_ref, wk_ref, wv_ref,
               attn_in_ref, att_ref, lse_ref, q_ref, kt_ref, kn_ref, vn_ref,
               kh_ref, vt_ref, s_ref):
    group, _ = tok_ref.shape
    width = wq_ref.shape[0]
    heads = width // HDIM
    lanes = q_ref.shape[0]
    tiles = group // TILE
    per_block = att_ref.shape[2] // TILE
    starts, ends = image_bounds(len_ref)

    def project(tile, _):
        rows = pl.ds(pl.multiple_of(tile * TILE, TILE), TILE)
        values = tok_ref[rows, :].astype(F32)
        centred = values - jnp.mean(values, axis=1, keepdims=True)
        variance = jnp.mean(centred * centred, axis=1, keepdims=True)
        normed = (centred * lax.rsqrt(variance + norm_eps) * gain_ref[...]).astype(BF16)
        attn_in_ref[rows, :] = normed
        q_ref[0:width, rows] = (dot_nt(wq_ref[...], normed).astype(BF16).astype(F32) * (1.0 / math.sqrt(HDIM))).astype(BF16)
        kt_ref[:, rows] = dot_nt(wk_ref[0:width, :], normed).astype(BF16)
        vt_ref[:, rows] = dot_nt(wv_ref[0:width, :], normed).astype(BF16)
        keys = dot_nt(normed, wk_ref[...]).astype(BF16).astype(F32)
        vn_ref[rows, :] = dot_nt(normed, wv_ref[...]).astype(BF16)
        place = tile * TILE + lax.broadcasted_iota(jnp.int32, (TILE, lanes), 0)
        lane = lax.broadcasted_iota(jnp.int32, (TILE, lanes), 1)
        here = tile * TILE + lax.broadcasted_iota(jnp.int32, (lanes - width, TILE), 1)
        row = lax.broadcasted_iota(jnp.int32, (lanes - width, TILE), 0)
        feature = jnp.zeros((lanes - width, TILE), F32)
        for image, (begin, end) in enumerate(zip(starts, ends)):
            keys = jnp.where((lane == width + image) & (place >= begin) & (place < end), 1.0, keys)
            feature = jnp.where((row == image) & ((here < begin) | (here >= end)), -BIG, feature)
        q_ref[width:lanes, rows] = feature.astype(BF16)
        kn_ref[rows, :] = keys.astype(BF16)
        for head in range(heads):
            kh_ref[head, rows, :] = jnp.where(head_mask(width, head, lanes), keys, 0.0).astype(BF16)
        return 0

    lax.fori_loop(0, tiles, project, 0)

    def attend(tile, _):
        columns = pl.ds(pl.multiple_of(tile * TILE, TILE), TILE)
        low, high = tile_range(starts, ends, tile)
        queries = q_ref[:, columns]

        def score(key_tile, tops):
            rows = pl.ds(pl.multiple_of(key_tile * TILE, TILE), TILE)
            result = []
            for head in range(heads):
                scores = dot_nn(kh_ref[head, rows, :], queries)
                s_ref[key_tile - low, head] = scores
                result.append(jnp.maximum(tops[head], jnp.max(scores, axis=0, keepdims=True)))
            return tuple(result)

        tops = lax.fori_loop(low, high, score, tuple(jnp.full((1, TILE), -3e38, F32) for _ in range(heads)))

        def gather(key_tile, carry):
            totals, parts = carry
            rows = pl.ds(pl.multiple_of(key_tile * TILE, TILE), TILE)
            new_totals, new_parts = [], []
            for head in range(heads):
                weight = jnp.exp(s_ref[key_tile - low, head] - tops[head])
                new_totals.append(totals[head] + jnp.sum(weight, axis=0, keepdims=True))
                new_parts.append(parts[head] + dot_nn(vt_ref[head * HDIM:(head + 1) * HDIM, rows], weight.astype(BF16)))
            return tuple(new_totals), tuple(new_parts)

        zero = tuple(jnp.zeros((1, TILE), F32) for _ in range(heads))
        zero_parts = tuple(jnp.zeros((HDIM, TILE), F32) for _ in range(heads))
        totals, parts = lax.fori_loop(low, high, gather, (zero, zero_parts))
        spot = pl.ds(pl.multiple_of(lax.rem(tile, per_block) * TILE, TILE), TILE)
        for head in range(heads):
            att_ref[tile // per_block, head * HDIM:(head + 1) * HDIM, spot] = (parts[head] / totals[head]).astype(BF16)
            lse_ref[head:head + 1, columns] = tops[head] + jnp.log(totals[head])
        return 0

    lax.fori_loop(0, tiles, attend, 0)


def bwd_kernel(len_ref, q_ref, kt_ref, kn_ref, vn_ref, lse_ref, att_ref, do_ref,
               out_ref, kh_ref, vh_ref, delta_ref, dq_ref, dk_ref, dv_ref):
    width, group = kt_ref.shape
    heads = width // HDIM
    lanes = kn_ref.shape[1]
    tiles = group // TILE
    per_block = do_ref.shape[2] // TILE
    starts, ends = image_bounds(len_ref)

    def prepare(tile, _):
        rows = pl.ds(pl.multiple_of(tile * TILE, TILE), TILE)
        spot = pl.ds(pl.multiple_of(lax.rem(tile, per_block) * TILE, TILE), TILE)
        keys, values = kn_ref[rows, :].astype(F32), vn_ref[rows, :].astype(F32)
        for head in range(heads):
            mask = head_mask(width, head, lanes)
            kh_ref[head, rows, :] = jnp.where(mask, keys, 0.0).astype(BF16)
            vh_ref[head, rows, :] = jnp.where(mask, values, 0.0).astype(BF16)[:, 0:width]
            part = slice(head * HDIM, (head + 1) * HDIM)
            delta_ref[head:head + 1, rows] = jnp.sum(
                do_ref[tile // per_block, part, spot].astype(F32) * att_ref[tile // per_block, part, spot].astype(F32),
                axis=0, keepdims=True)
        dq_ref[:, rows] = jnp.zeros((width, TILE), F32)
        return 0

    lax.fori_loop(0, tiles, prepare, 0)

    def key_step(key_tile, _):
        rows = pl.ds(pl.multiple_of(key_tile * TILE, TILE), TILE)
        low, high = tile_range(starts, ends, key_tile)
        dk_ref[...] = jnp.zeros_like(dk_ref)
        dv_ref[...] = jnp.zeros_like(dv_ref)

        def query_step(tile, _):
            columns = pl.ds(pl.multiple_of(tile * TILE, TILE), TILE)
            spot = pl.ds(pl.multiple_of(lax.rem(tile, per_block) * TILE, TILE), TILE)
            queries = q_ref[:, columns]
            grads = do_ref[tile // per_block, :, spot]
            for head in range(heads):
                part = slice(head * HDIM, (head + 1) * HDIM)
                scores = dot_nn(kh_ref[head, rows, :], queries)
                probs = jnp.exp(scores - lse_ref[head:head + 1, columns])
                grad_weights = dot_nn(vh_ref[head, rows, :], grads)
                grad_scores = (probs * (grad_weights - delta_ref[head:head + 1, columns])).astype(BF16)
                dv_ref[part, :] += dot_nt(grads[part, :], probs.astype(BF16))
                dk_ref[part, :] += dot_nt(queries[part, :], grad_scores)
                dq_ref[part, columns] += dot_nn(kt_ref[part, rows], grad_scores)
            return 0

        lax.fori_loop(low, high, query_step, 0)
        out_ref[width:2 * width, rows] = dk_ref[...].astype(BF16)
        out_ref[2 * width:3 * width, rows] = dv_ref[...].astype(BF16)
        return 0

    lax.fori_loop(0, tiles, key_step, 0)
    out_ref[0:width, :] = (dq_ref[...] * (1.0 / math.sqrt(HDIM))).astype(BF16)


VM = pl.BlockSpec(memory_space=pltpu.VMEM)
SM = pl.BlockSpec(memory_space=pltpu.SMEM)
LIMIT = 60 * 2**20


def attn_fwd(lengths, tokens, gain, wq, wk, wv, blocks):
    group, model = tokens.shape
    width = wq.shape[0]
    lanes = wk.shape[0]
    heads = width // HDIM
    tiles = group // TILE
    S = jax.ShapeDtypeStruct
    return pl.pallas_call(
        fwd_kernel,
        out_shape=(S((group, model), BF16), S((blocks, width, group // blocks), BF16), S((8, group), F32),
                   S((lanes, group), BF16), S((width, group), BF16), S((group, lanes), BF16), S((group, lanes), BF16)),
        in_specs=[SM] + [VM] * 5, out_specs=(VM,) * 7,
        scratch_shapes=[pltpu.VMEM((heads, group, lanes), BF16), pltpu.VMEM((width, group), BF16),
                        pltpu.VMEM((tiles, heads, TILE, TILE), F32)],
        compiler_params=pltpu.CompilerParams(vmem_limit_bytes=LIMIT),
        cost_estimate=pl.CostEstimate(flops=8 * 10**9, bytes_accessed=10**7, transcendentals=4 * 10**6),
        name="attend_forward",
    )(lengths, tokens, gain, wq, wk, wv)


def attn_bwd(lengths, q, kt, kn, vn, lse, att, do):
    width, group = kt.shape
    lanes = kn.shape[1]
    heads = width // HDIM
    S = jax.ShapeDtypeStruct
    return pl.pallas_call(
        bwd_kernel,
        out_shape=S((3 * width, group), BF16),
        in_specs=[SM] + [VM] * 7, out_specs=VM,
        scratch_shapes=[pltpu.VMEM((heads, group, lanes), BF16), pltpu.VMEM((heads, group, width), BF16),
                        pltpu.VMEM((8, group), F32), pltpu.VMEM((width, group), F32),
                        pltpu.VMEM((width, TILE), F32), pltpu.VMEM((width, TILE), F32)],
        compiler_params=pltpu.CompilerParams(vmem_limit_bytes=LIMIT),
        cost_estimate=pl.CostEstimate(flops=16 * 10**9, bytes_accessed=10**7, transcendentals=4 * 10**6),
        name="attend_backward",
    )(lengths, q, kt, kn, vn, lse, att, do)


def matmul(left, right):
    return jnp.dot(left, right, preferred_element_type=F32)


def inner_rows(left, right):
    return lax.dot_general(left, right, (((0,), (0,)), ((), ())), preferred_element_type=F32)


def times_transposed(left, right):
    return lax.dot_general(left, right, (((1,), (1,)), ((), ())), preferred_element_type=F32)


def norm_rows(values):
    mean_row = jnp.mean(values, axis=-1, keepdims=True)
    centred = values - mean_row
    variance = jnp.mean(centred * centred, axis=-1, keepdims=True)
    root_inv = lax.rsqrt(variance + norm_eps)
    return (centred * root_inv, root_inv)


def norm_back(grad_scaled, normed, root_inv):
    first_mean = jnp.mean(grad_scaled, axis=-1, keepdims=True)
    second_mean = jnp.mean(grad_scaled * normed, axis=-1, keepdims=True)
    return root_inv * (grad_scaled - first_mean - normed * second_mean)


def gelu_parts(pre_act):
    normal_cdf = 0.5 * (1.0 + lax.erf(pre_act * 0.7071067811865476))
    density = jnp.exp(-0.5 * pre_act * pre_act) * 0.3989422804014327
    return (pre_act * normal_cdf, normal_cdf + pre_act * density)


def flip(value, bit):
    size = lax.axis_size("narrow")
    return lax.ppermute(value, "narrow", [(i, i ^ bit) for i in range(size)])


def swap_wide(rows, experts):
    shape = rows.shape
    return lax.all_to_all(
        rows.reshape(experts, -1, shape[1]), "wide", split_axis=0, concat_axis=0, tiled=True
    ).reshape(shape)


def swap_narrow(blocks):
    return lax.all_to_all(blocks, "narrow", split_axis=0, concat_axis=0, tiled=True)


def local(
    tokens,
    cotangent,
    lengths,
    routes,
    capacity_slots,
    first_gain,
    second_gain,
    query_weight,
    key_weight,
    value_weight,
    out_weight,
    router_weight,
    expert_in,
    expert_out,
):
    experts = lax.axis_size("wide")
    narrow = lax.axis_size("narrow")
    own_expert = lax.axis_index("wide")
    own_block = lax.axis_index("narrow")
    block_rows, model = cotangent.shape
    capacity = (42 * block_rows + 20 * experts - 1) // (20 * experts)
    slots = -(-capacity // 8) * 8
    width = query_weight.shape[1]

    in_here, out_here = expert_in[0], expert_out[0]
    out_there = flip(out_here, 2)
    in_there = flip(in_here, 2)
    out_parts = [out_here, flip(out_here, 1), out_there, flip(out_there, 1)]
    in_parts = [in_here, flip(in_here, 1), in_there, flip(in_there, 1)]
    out_full = lax.all_gather(out_weight, "narrow", axis=0, tiled=True)

    place = jnp.where(capacity_slots < capacity, routes * slots + capacity_slots, experts * slots)
    slot_ids = jnp.arange(experts * slots, dtype=jnp.int32)
    select = (
        (place[:, 0:1] == slot_ids[None, :]) | (place[:, 1:2] == slot_ids[None, :])
    ).astype(BF16)
    cot_rows = swap_wide(inner_rows(select, cotangent).astype(BF16), experts)

    query_t, key_t, value_t = query_weight.T, key_weight.T, value_weight.T
    lanes = -(-(width + lengths.shape[1]) // 128) * 128
    pad = ((0, lanes - width), (0, 0))
    attn_in, att, lse, q_keep, kt_keep, kn_keep, vn_keep = attn_fwd(
        lengths, tokens, first_gain[None], query_t, jnp.pad(key_t, pad), jnp.pad(value_t, pad), narrow
    )
    att_own = swap_narrow(att).reshape(narrow * width, block_rows)
    own_tokens = lax.dynamic_slice_in_dim(tokens, own_block * block_rows, block_rows, 0).astype(F32)
    hidden_one = own_tokens + inner_rows(att_own, out_full)
    normed_two, root_two = norm_rows(hidden_one)
    moe_in = (normed_two * second_gain).astype(BF16)
    rows = swap_wide(inner_rows(select, moe_in).astype(BF16), experts)

    logits = matmul(rows, router_weight)
    logit_exp = jnp.exp(logits - jnp.max(logits, axis=1, keepdims=True))
    probs = logit_exp / jnp.sum(logit_exp, axis=1, keepdims=True)
    mine = (jnp.arange(experts, dtype=jnp.int32) == own_expert).astype(F32)[None, :]
    gate = jnp.sum(probs * mine, axis=1, keepdims=True)
    grad_gate = jnp.zeros_like(gate)
    act_parts, pre_grads = [], []
    for w_in, w_out in zip(in_parts, out_parts):
        back = times_transposed(cot_rows, w_out).astype(BF16)
        activated, slope = gelu_parts(matmul(rows, w_in))
        act_low = activated.astype(BF16)
        act_parts.append(act_low)
        grad_gate = grad_gate + jnp.sum(act_low.astype(F32) * back.astype(F32), axis=1, keepdims=True)
        pre_grads.append((gate * back.astype(F32) * slope).astype(BF16))
    grad_logits = (grad_gate * probs * (mine - gate)).astype(BF16)
    grad_sum = times_transposed(grad_logits, router_weight)
    for pre_grad, w_in in zip(pre_grads, in_parts):
        grad_sum = grad_sum + times_transposed(pre_grad, w_in)
    grad_home = swap_wide(grad_sum.astype(BF16), experts)
    result = sum(matmul(act, w_out) for act, w_out in zip(act_parts, out_parts))
    result_home = swap_wide((gate * result).astype(BF16), experts)
    grad_result = (gate * cot_rows.astype(F32)).astype(BF16)
    router_part = inner_rows(rows, grad_logits)
    out_grads = [inner_rows(act, grad_result) for act in act_parts]
    in_grads = [inner_rows(rows, pre_grad) for pre_grad in pre_grads]

    def sum_narrow(parts):
        one, three = flip(parts[1].astype(BF16), 1), flip(parts[3].astype(BF16), 1)
        keep = parts[0] + one.astype(F32)
        send = (parts[2] + three.astype(F32)).astype(BF16)
        return keep + flip(send, 2).astype(F32)

    out_grad, in_grad = sum_narrow(out_grads)[None], sum_narrow(in_grads)[None]

    grad_moe_in = matmul(select, grad_home)
    mixed = hidden_one + matmul(select, result_home)
    block_output = mixed.astype(BF16)
    second_part = jnp.sum(grad_moe_in * normed_two, axis=0)
    grad_hidden = cotangent.astype(F32) + norm_back(grad_moe_in * second_gain, normed_two, root_two)
    grad_branch = grad_hidden.astype(BF16)
    grad_att = times_transposed(out_full, grad_branch).astype(BF16)
    grad_heads = swap_narrow(grad_att.reshape(narrow, width, block_rows))
    out_part = matmul(att_own, grad_branch)
    out_weight_grad = lax.psum(
        lax.psum_scatter(out_part, "narrow", scatter_dimension=0, tiled=True), "wide"
    )
    small = lax.psum(
        jnp.concatenate([router_part, second_part[:, None]], axis=1), ("wide", "narrow")
    )

    grad_qkv = attn_bwd(lengths, q_keep, kt_keep, kn_keep, vn_keep, lse, att, grad_heads)
    qkv_t = jnp.concatenate([query_t, key_t, value_t], axis=0)
    grad_attn_in = inner_rows(grad_qkv, qkv_t).astype(BF16).reshape(narrow, block_rows, model)

    def block_of(bits):
        return lax.dynamic_index_in_dim(grad_attn_in, own_block ^ bits, 0, keepdims=False)

    grad_rows_att = sum_narrow([block_of(bits).astype(F32) for bits in range(4)])
    qkv_part = lax.dot_general(
        attn_in, grad_qkv, (((0,), (1,)), ((), ())), preferred_element_type=F32
    )
    first_part = jnp.sum(qkv_part * qkv_t.T.astype(F32), axis=1) / first_gain
    qkv_grad = lax.psum(qkv_part, "wide")
    first = lax.psum(first_part, ("wide", "narrow"))
    own_normed, own_root = norm_rows(own_tokens)
    token_grad = grad_hidden + norm_back(grad_rows_att * first_gain, own_normed, own_root)

    def own_share(value):
        size = value.shape[0] // narrow
        return lax.dynamic_slice_in_dim(value, own_block * size, size, 0)

    small = own_share(small)
    return (
        block_output,
        token_grad,
        own_share(first),
        small[:, experts],
        qkv_grad[:, 0:width],
        qkv_grad[:, width:2 * width],
        qkv_grad[:, 2 * width:3 * width],
        out_weight_grad,
        small[:, 0:experts],
        in_grad,
        out_grad,
    )


def solution(mesh):
    in_specs = (
        P("wide", None),
        P(("wide", "narrow"), None),
        P("wide", None),
        P(("wide", "narrow"), None),
        P(("wide", "narrow"), None),
        P(),
        P(),
        P(None, "narrow"),
        P(None, "narrow"),
        P(None, "narrow"),
        P("narrow", None),
        P(),
        P("wide", None, "narrow"),
        P("wide", "narrow", None),
    )
    out_specs = (
        P(("wide", "narrow"), None),
        P(("wide", "narrow"), None),
        P("narrow"),
        P("narrow"),
        P(None, "narrow"),
        P(None, "narrow"),
        P(None, "narrow"),
        P("narrow", None),
        P("narrow", None),
        P("wide", None, "narrow"),
        P("wide", "narrow", None),
    )
    return jax.shard_map(local, mesh=mesh, in_specs=in_specs, out_specs=out_specs, check_vma=False)
```

time: 1140 us -> 483 us (0.42)
  waiting for transfers between devices: 435 us -> 166 us
  local copies, waits for them, and re-layouts: 195 us -> 18.4 us
  matrix products: 213 us -> 113 us
  other arithmetic: 108 us -> 20.5 us
  blocking collectives: 134 us -> 51.8 us
  Pallas kernels: 0 us -> 56.6 us
  starting transfers between devices: 12.8 us -> 36.5 us
  loops' own time: 13.6 us -> 0 us
    reduce_scatter x4 -> x1, waiting for transfers between devices: 172 us -> 0.01 us  [local(): lax.psum_scatter(out_part, 'narrow', scatter_dimension=0, tiled=True)]
    all_gather x3 -> x1, waiting for transfers between devices: 118 us -> 0.01 us  [local(): out_full = lax.all_gather(out_weight, 'narrow', axis=0, tiled=True)]
    dot_general x35 -> x13, matrix products: 154 us -> 36.5 us  [the longest x12 33.2 us: matmul(): return jnp.dot(left, right, preferred_element_type=F32)]
    all_to_all x2 -> x0, blocking collectives: 88.3 us -> none  [the longest x1 45.1 us: local(): lax.all_to_all(padded_in[slot_table], 'wide', split_axis=0, concat_axis=0...]
    dynamic_update_slice x12 -> x0, local copies, waits for them, and re-layouts: 58.2 us -> none  [the longest x4 29.1 us: block_back(): lax.dynamic_update_slice_in_dim(grad_values, lax.dynamic_slice_in_dim(gra...]
    pallas_call x0 -> x2, Pallas kernels: none -> 56.6 us  [the longest x1 28.6 us: attn_fwd(): pl.pallas_call(fwd_kernel, out_shape=(S((group, model), BF16), S((blocks,...]
    ppermute x0 -> x15, waiting for transfers between devices: none -> 48 us  [flip(): return lax.ppermute(value, 'narrow', [(i, i ^ bit) for i in range(size)])]
    convert_element_type x15 -> x4, other arithmetic: 50.3 us -> 3.06 us  [the longest x1 2.59 us: sum_narrow(): send = (parts[2] + three.astype(F32)).astype(BF16)]
  transfers between devices with their start and end apart: 11 -> 24, of which waited for: 9 -> 8; matrix products, arithmetic and copies ran while one was open for 23% -> 24% of each run, Pallas kernels for 0% -> 12%
where the time goes in v1:
time: 483 us; the launch traced here: 477 us
  waiting for transfers between devices  166 us (34%)
  matrix products  113 us (23%)
  Pallas kernels  56.6 us (12%)
  blocking collectives  51.8 us (11%)
  starting transfers between devices  36.5 us (8%)
  other arithmetic  20.5 us (4%)
  local copies, waits for them, and re-layouts  18.4 us (4%)
  between operations  14.7 us (3%)
    all_to_all x4, waiting for transfers between devices, swap_wide(): lax.all_to_all(rows.reshape(experts, -1, shape[1]), 'wide', split_axis=0,...  57.3 us
    psum x1, blocking collectives, local(): first = lax.psum(first_part, ('wide', 'narrow'))  51.8 us
    ppermute x15, waiting for transfers between devices, flip(): return lax.ppermute(value, 'narrow', [(i, i ^ bit) for i in range(size)])  48 us
    dot_general x13, matrix products, inner_rows(): lax.dot_general(left, right, (((0,), (0,)), ((), ())), preferred_element_...  40.8 us
    psum x1, waiting for transfers between devices, local(): qkv_grad = lax.psum(qkv_part, 'wide')  38.3 us
    dot_general x10, matrix products, times_transposed(): lax.dot_general(left, right, (((1,), (1,)), ((), ())), preferred_element_...  35.8 us
    dot_general x12, matrix products, matmul(): return jnp.dot(left, right, preferred_element_type=F32)  33.2 us
    pallas_call x1, Pallas kernels, attn_fwd(): pl.pallas_call(fwd_kernel, out_shape=(S((group, model), BF16), S((blocks,...  28.6 us
  transfers between devices with their start and end apart: 24, of which 8 were waited for; matrix products, arithmetic and copies ran while one was open for 24% of the time, Pallas kernels for 12%

profile of v1, /device:TPU:0, one launch (start us, length us, event | category | flops | bytes accessed | tf_op | source)
XLA Modules:
  0.0 477.3 jit_solution(3488794186484997598)
XLA Ops:
  12.7 28.6 %attend_forward.1 = (bf16[2048,768]{1,0:T(8,128)(2,1)}, bf16[4,192,512]{2,1,0:T(8,128)(2,1)}, f32[8,2048]{1,0:T(8,128)}, bf16[256,2048]{1,0:T(8,128)(2,1)}, bf16...) custom-call(s32[1,8]{1,0:T(1,128)} %len_ref.3, bf16[2048,768]{1,0:T(8,128)(2,1)} %tok_ref.1, ...), custom_call_target="tpu_custom_call" | custom-call | flops 8000000000 | bytes 10000000 | tf_op jit(solution)/shard_map/attend_forward/pallas_call | solution.py:195
  41.2 4.2 all-to-all-start
  45.5 11.6 %all-to-all-done = bf16[4,192,512]{2,1,0:T(8,128)(2,1)S(1)} async-done(((bf16[4,192,512]{2,1,0:T(8,128)(2,1)}), bf16[4,192,512]{2,1,0:T(8,128)(2,1)S(1)}, u32[]{:S(2)}, u32[]{:S(2)}) %all-to-all-start) | async-done | bytes 786464 | tf_op jit(solution)/shard_map/all_to_all | solution.py:271
  57.1 2.7 fusion.71
  60.2 2.7 convolution_convert_fusion.1
  62.9 7.9 %all-to-all-start.1 = ((bf16[8,136,768]{2,1,0:T(8,128)(2,1)}), bf16[8,136,768]{2,1,0:T(8,128)(2,1)S(1)}, u32[]{:S(2)}, u32[]{:S(2)}) async-start(bf16[8,136,768]{2,1,0:T(8,128)(2,1)} %bitcast.139), calls=%async_computation.1 | async-start | bytes 3342336 | tf_op jit(solution)/shard_map/all_to_all | solution.py:265
  73.2 36.5 %all-to-all-done.1 = bf16[8,136,768]{2,1,0:T(8,128)(2,1)S(1)} async-done(((bf16[8,136,768]{2,1,0:T(8,128)(2,1)}), bf16[8,136,768]{2,1,0:T(8,128)(2,1)S(1)}, u32[]{:S(2)}, u32[]{:S(2)}) %all-to-all-start.1) | async-done | bytes 1671200 | tf_op jit(solution)/shard_map/all_to_all | solution.py:265
  109.6 3.9 all-to-all-start.3
  119.1 23.7 %collective-permute-done.2 = bf16[768,768]{1,0:T(8,128)(2,1)} collective-permute-done((bf16[768,768]{1,0:T(8,128)(2,1)}, bf16[768,768]{1,0:T(8,128)(2,1)}, u32[]{:S(2)}, u32[]{:S(2)}) %collective-permute-start.2) | collective-permute-done | bytes 1179680 | tf_op jit(solution)/shard_map/ppermute | solution.py:260
  142.8 24.0 %collective-permute-done.3 = bf16[768,768]{1,0:T(8,128)(2,1)} collective-permute-done((bf16[768,768]{1,0:T(8,128)(2,1)}, bf16[768,768]{1,0:T(8,128)(2,1)}, u32[]{:S(2)}, u32[]{:S(2)}) %collective-permute-start.3) | collective-permute-done | bytes 1179680 | tf_op jit(solution)/shard_map/ppermute | solution.py:260
  167.5 3.2 fusion.67
  170.7 5.9 %fusion.4 = (f32[1088]{0:T(1024)S(1)}, bf16[1088,768]{1,0:T(8,128)(2,1)}, bf16[1088,768]{1,0:T(8,128)(2,1)S(1)}) fusion(f32[1088,768]{1,0:T(8,128)} %fusion.67, f32[1088]{0:T(1024)S(1)} %multiply_reduce_fusion.4, bf16[1088,768]{1,0:T(8,128)(2,1)S(1)} %bitcast.126, bf16[1,768,768]{2,1,0:T(8,128)(2,1)} %param.27), kind=kOutput, calls=%fused_computation.29 | convolution fusion | flops 1298496512 | bytes 9544192 | tf_op jit(solution)/shard_map/dot_general | solution.py:235
  176.6 3.3 fusion.74
  180.0 5.4 %fusion.10 = (f32[1088]{0:T(1024)S(1)}, bf16[1088,768]{1,0:T(8,128)(2,1)}, bf16[1088,768]{1,0:T(8,128)(2,1)S(1)}) fusion(f32[1088,768]{1,0:T(8,128)S(1)} %fusion.74, f32[1088]{0:T(1024)S(1)} %multiply_reduce_fusion.4, bf16[1088,768]{1,0:T(8,128)(2,1)S(1)} %bitcast.127, bf16[768,768]{1,0:T(8,128)(2,1)} %collective-permute-done.3), kind=kOutput, calls=%fused_computation.35 | convolution fusion | flops 1298496512 | bytes 9544192 | tf_op jit(solution)/shard_map/dot_general | solution.py:235
  186.9 2.8 fusion.73
  189.7 2.8 fusion.75
  192.5 5.3 %fusion.7 = (f32[1088]{0:T(1024)S(1)}, bf16[1088,768]{1,0:T(8,128)(2,1)}, bf16[1088,768]{1,0:T(8,128)(2,1)S(1)}) fusion(f32[1088,768]{1,0:T(8,128)S(1)} %fusion.73, f32[1088]{0:T(1024)S(1)} %multiply_reduce_fusion.4, bf16[1088,768]{1,0:T(8,128)(2,1)S(1)} %bitcast.128, bf16[768,768]{1,0:T(8,128)(2,1)} %collective-permute-done.1), kind=kOutput, calls=%fused_computation.32 | convolution fusion | flops 1298496512 | bytes 9544192 | tf_op jit(solution)/shard_map/dot_general | solution.py:235
  197.8 5.7 %fusion.13 = (f32[1088]{0:T(1024)S(1)}, bf16[1088,768]{1,0:T(8,128)(2,1)}, bf16[1088,768]{1,0:T(8,128)(2,1)S(1)}) fusion(f32[1088,768]{1,0:T(8,128)S(1)} %fusion.75, f32[1088]{0:T(1024)S(1)} %multiply_reduce_fusion.4, bf16[1088,768]{1,0:T(8,128)(2,1)S(1)} %bitcast.129, bf16[768,768]{1,0:T(8,128)(2,1)} %collective-permute-done.5), kind=kOutput, calls=%fused_computation.38 | convolution fusion | flops 1298496512 | bytes 9544192 | tf_op jit(solution)/shard_map/dot_general | solution.py:235
  203.6 2.8 convolution_convert_fusion.9
  206.4 2.8 convolution_convert_fusion.10
  209.8 2.8 fusion.76
  212.6 2.8 fusion
  215.4 4.0 fusion.3
  219.4 5.7 %all-to-all-start.4 = ((bf16[8,136,768]{2,1,0:T(8,128)(2,1)}), bf16[8,136,768]{2,1,0:T(8,128)(2,1)}, u32[]{:S(2)}, u32[]{:S(2)}) async-start(bf16[8,136,768]{2,1,0:T(8,128)(2,1)} %bitcast.138), calls=%async_computation.4 | async-start | bytes 3342336 | tf_op jit(solution)/shard_map/all_to_all | solution.py:265
  226.8 2.8 convolution_convert_fusion.7
  229.8 2.8 convolution_convert_fusion.8
  234.4 2.9 convolution_add_fusion.5
  237.3 2.8 convolution_add_fusion.4
  240.1 4.1 fusion.2
  244.2 20.8 %all-to-all-done.4 = bf16[8,136,768]{2,1,0:T(8,128)(2,1)} async-done(((bf16[8,136,768]{2,1,0:T(8,128)(2,1)}), bf16[8,136,768]{2,1,0:T(8,128)(2,1)}, u32[]{:S(2)}, u32[]{:S(2)}) %all-to-all-start.4) | async-done | bytes 1671200 | tf_op jit(solution)/shard_map/all_to_all | solution.py:265
  265.0 3.4 multiply_reduce_fusion
  271.8 4.9 %fusion.78 = f32[768,768]{1,0:T(8,128)} fusion(bf16[1088,768]{1,0:T(8,128)(2,1)S(1)} %bitcast.123, bf16[1088,768]{1,0:T(8,128)(2,1)} %copy-done.33), kind=kOutput, calls=%fused_computation.152 | convolution fusion | flops 1283457024 | bytes 5701632 | tf_op jit(solution)/shard_map/dot_general | solution.py:231
  278.4 3.2 fusion.79
  285.7 4.2 all-to-all-start.5
  289.9 4.7 add_convert_fusion.1
  296.6 4.1 add_convert_fusion
  300.8 9.7 %all-to-all-done.5.do_ref = bf16[4,192,512]{2,1,0:T(8,128)(2,1)} async-done(((bf16[4,192,512]{2,1,0:T(8,128)(2,1)}), bf16[4,192,512]{2,1,0:T(8,128)(2,1)}, u32[]{:S(2)}, u32[]{:S(2)}) %all-to-all-start.5) | async-done | bytes 786464 | tf_op jit(solution)/shard_map/all_to_all | solution.py:271
  310.5 4.3 all-to-all-start.2
  315.1 28.0 %attend_backward.1 = bf16[576,2048]{1,0:T(8,128)(2,1)} custom-call(s32[1,8]{1,0:T(1,128)} %len_ref.3, bf16[256,2048]{1,0:T(8,128)(2,1)} %get-tuple-element.19.q_ref, bf16[192,2048]{1,0:T(8,128)(2,1)} %get-tuple-element.20.kt_ref, bf16[2048,256]{1,0:T(8,128)(2,1)} %get-tuple-element.21.kn_ref, bf16[2048,256]{1,0:T(8,128)(2,1)} %get-tuple-element.22.vn_ref, ...), custom_call_target="tpu_custom_call" | custom-call | flops 16000000000 | bytes 10000000 | tf_op jit(solution)/shard_map/attend_backward/pallas_call | solution.py:213
  343.2 4.5 convolution_convert_fusion.2
  351.1 3.3 fusion.37
  354.4 3.7 add_bitcast_fusion.1
  361.1 3.5 add_bitcast_fusion
  364.6 3.8 add_convert_fusion.2
  368.4 51.8 %all-reduce.2 = (f32[768]{0:T(1024)S(1)}, f32[768,9]{0,1:T(8,128)S(1)}) all-reduce(f32[768]{0:T(1024)S(1)} %div.45, f32[768,9]{0,1:T(8,128)S(1)} %pad_maximum_fusion.2), channel_id=1, replica_groups=mesh['wide'=8,'narrow'=4] {'wide','narrow'}, use_global_device_ids=true, to_apply=%region_16.17 | all-reduce | flops 7680 | bytes 61440 | tf_op jit(solution)/shard_map/psum | solution.py:389
  424.7 3.8 fusion.41
  428.5 38.3 %all-reduce.6.cloned.1.call-done = (f32[768,576]{0,1:T(8,128)}, f32[192,768]{1,0:T(8,128)}) async-done(((f32[768,576]{0,1:T(8,128)}, f32[192,768]{1,0:T(8,128)}), (f32[768,576]{0,1:T(8,128)}, f32[192,768]{1,0:T(8,128)})) %all-reduce.6.cloned.1.call-update) | async-done | bytes 2359312 | tf_op jit(solution)/shard_map/psum | solution.py:388
  466.8 2.7 fusion.69
  (153 shorter events, 43.6 us)
Async XLA Ops:
  7.2 159.6 %copy-start = (bf16[768,8]{0,1:T(8,128)(2,1)S(1)}, bf16[768,8]{0,1:T(8,128)(2,1)}, u32[]{:S(2)}) copy-start(bf16[768,8]{0,1:T(8,128)(2,1)} %param.25) | copy-start | bytes 36868
  7.2 49.9 %all-gather.2.cloned.1.call-start = ((), (), s32[]{:S(2)}) async-start(), calls=%async_computation.7 | async-start | bytes 1474560 | tf_op jit(solution)/shard_map/all_gather | solution.py:304
  12.7 32.8 %copy-start.20 = (s32[512,2]{0,1:T(2,128)S(1)}, s32[512,2]{0,1:T(2,128)}, u32[]{:S(2)}) copy-start(s32[512,2]{0,1:T(2,128)} %param.18) | copy-start | bytes 12292
  12.7 32.8 %copy-start.21 = (s32[512,2]{0,1:T(2,128)S(1)}, s32[512,2]{0,1:T(2,128)}, u32[]{:S(2)}) copy-start(s32[512,2]{0,1:T(2,128)} %param.17) | copy-start | bytes 12292
  41.2 15.9 %all-to-all-start = ((bf16[4,192,512]{2,1,0:T(8,128)(2,1)}), bf16[4,192,512]{2,1,0:T(8,128)(2,1)S(1)}, u32[]{:S(2)}, u32[]{:S(2)}) async-start(bf16[4,192,512]{2,1,0:T(8,128)(2,1)} %get-tuple-element.18.att_ref), calls=%async_computation | async-start | bytes 1572864 | tf_op jit(solution)/shard_map/all_to_all | solution.py:271
  62.9 7.9 %copy-start.13 = (bf16[512,768]{1,0:T(8,128)(2,1)S(1)}, bf16[512,768]{1,0:T(8,128)(2,1)}, u32[]{:S(2)}) copy-start(bf16[512,768]{1,0:T(8,128)(2,1)} %param.15) | copy-start | bytes 2359300
  62.9 46.8 %all-to-all-start.1 = ((bf16[8,136,768]{2,1,0:T(8,128)(2,1)}), bf16[8,136,768]{2,1,0:T(8,128)(2,1)S(1)}, u32[]{:S(2)}, u32[]{:S(2)}) async-start(bf16[8,136,768]{2,1,0:T(8,128)(2,1)} %bitcast.139), calls=%async_computation.1 | async-start | bytes 3342336 | tf_op jit(solution)/shard_map/all_to_all | solution.py:265
  109.6 61.1 %all-to-all-start.3 = ((bf16[8,136,768]{2,1,0:T(8,128)(2,1)}), bf16[8,136,768]{2,1,0:T(8,128)(2,1)S(1)}, u32[]{:S(2)}, u32[]{:S(2)}) async-start(bf16[8,136,768]{2,1,0:T(8,128)(2,1)} %bitcast.137), calls=%async_computation.3 | async-start | bytes 3342336 | tf_op jit(solution)/shard_map/all_to_all | solution.py:265
  113.5 29.3 %collective-permute-start.2 = (bf16[768,768]{1,0:T(8,128)(2,1)}, bf16[768,768]{1,0:T(8,128)(2,1)}, u32[]{:S(2)}, u32[]{:S(2)}) collective-permute-start(bf16[768,768]{1,0:T(8,128)(2,1)} %bitcast.155), channel_id=1, source_target_pairs={{0,2},{1,3},{2,0},{3,1},{4,6},{5,7},{6,4},{7,5},{8,10},{9,11},{10,... | collective-permute-start | bytes 3538952 | tf_op jit(solution)/shard_map/ppermute | solution.py:260
  114.2 52.6 %collective-permute-start.3 = (bf16[768,768]{1,0:T(8,128)(2,1)}, bf16[768,768]{1,0:T(8,128)(2,1)}, u32[]{:S(2)}, u32[]{:S(2)}) collective-permute-start(bf16[768,768]{1,0:T(8,128)(2,1)} %bitcast.157), channel_id=1, source_target_pairs={{0,2},{1,3},{2,0},{3,1},{4,6},{5,7},{6,4},{7,5},{8,10},{9,11},{10,... | collective-permute-start | bytes 3538952 | tf_op jit(solution)/shard_map/ppermute | solution.py:260
  115.6 71.3 %collective-permute-start = (bf16[768,768]{1,0:T(8,128)(2,1)}, bf16[768,768]{1,0:T(8,128)(2,1)}, u32[]{:S(2)}, u32[]{:S(2)}) collective-permute-start(bf16[768,768]{1,0:T(8,128)(2,1)} %bitcast.156), channel_id=1, source_target_pairs={{0,1},{1,0},{2,3},{3,2},{4,5},{5,4},{6,7},{7,6},{8,9},{9,8},{10,11... | collective-permute-start | bytes 3538952 | tf_op jit(solution)/shard_map/ppermute | solution.py:260
  115.6 76.9 %collective-permute-start.1 = (bf16[768,768]{1,0:T(8,128)(2,1)}, bf16[768,768]{1,0:T(8,128)(2,1)}, u32[]{:S(2)}, u32[]{:S(2)}) collective-permute-start(bf16[768,768]{1,0:T(8,128)(2,1)} %bitcast.158), channel_id=1, source_target_pairs={{0,1},{1,0},{2,3},{3,2},{4,5},{5,4},{6,7},{7,6},{8,9},{9,8},{10,11... | collective-permute-start | bytes 3538952 | tf_op jit(solution)/shard_map/ppermute | solution.py:260
  116.1 51.4 %copy-start.22 = (bf16[1,768,768]{2,1,0:T(8,128)(2,1)S(1)}, bf16[1,768,768]{2,1,0:T(8,128)(2,1)}, u32[]{:S(2)}) copy-start(bf16[1,768,768]{2,1,0:T(8,128)(2,1)} %param.26) | copy-start | bytes 3538948
  142.8 46.9 %collective-permute-start.4 = (bf16[768,768]{1,0:T(8,128)(2,1)}, bf16[768,768]{1,0:T(8,128)(2,1)}, u32[]{:S(2)}, u32[]{:S(2)}) collective-permute-start(bf16[768,768]{1,0:T(8,128)(2,1)} %collective-permute-done.2), channel_id=1, source_target_pairs={{0,1},{1,0},{2,3},{3,2},{4,5},{5,4},{6,7},{7,6},{8,9},{9,8},{10,11... | collective-permute-start | bytes 3538952 | tf_op jit(solution)/shard_map/ppermute | solution.py:260
  166.8 31.0 %collective-permute-start.5 = (bf16[768,768]{1,0:T(8,128)(2,1)}, bf16[768,768]{1,0:T(8,128)(2,1)}, u32[]{:S(2)}, u32[]{:S(2)}) collective-permute-start(bf16[768,768]{1,0:T(8,128)(2,1)} %collective-permute-done.3), channel_id=1, source_target_pairs={{0,1},{1,0},{2,3},{3,2},{4,5},{5,4},{6,7},{7,6},{8,9},{9,8},{10,11... | collective-permute-start | bytes 3538952 | tf_op jit(solution)/shard_map/ppermute | solution.py:260
  176.6 8.8 %copy-start.33 = (bf16[1088,768]{1,0:T(8,128)(2,1)}, bf16[1088,768]{1,0:T(8,128)(2,1)S(1)}, u32[]{:S(2)}) copy-start(bf16[1088,768]{1,0:T(8,128)(2,1)S(1)} %get-tuple-element.44) | copy-start | bytes 5013508
  180.0 5.4 %copy-start.23 = (bf16[1,768,768]{2,1,0:T(8,128)(2,1)S(1)}, bf16[1,768,768]{2,1,0:T(8,128)(2,1)}, u32[]{:S(2)}) copy-start(bf16[1,768,768]{2,1,0:T(8,128)(2,1)} %param.26) | copy-start | bytes 3538948
  185.4 24.4 %copy-start.32 = (bf16[1088,768]{1,0:T(8,128)(2,1)}, bf16[1088,768]{1,0:T(8,128)(2,1)S(1)}, u32[]{:S(2)}) copy-start(bf16[1088,768]{1,0:T(8,128)(2,1)S(1)} %get-tuple-element.45) | copy-start | bytes 5013508
  219.4 45.6 %all-to-all-start.4 = ((bf16[8,136,768]{2,1,0:T(8,128)(2,1)}), bf16[8,136,768]{2,1,0:T(8,128)(2,1)}, u32[]{:S(2)}, u32[]{:S(2)}) async-start(bf16[8,136,768]{2,1,0:T(8,128)(2,1)} %bitcast.138), calls=%async_computation.4 | async-start | bytes 3342336 | tf_op jit(solution)/shard_map/all_to_all | solution.py:265
  225.1 129.3 %reduce-scatter.2.cloned.1.call-start = ((), (), s32[]{:S(2)}) async-start(), calls=%async_computation.8 | async-start | bytes 2949120 | tf_op jit(solution)/shard_map/reduce_scatter | solution.py:370
  225.3 64.6 %collective-permute-start.10 = (bf16[768,768]{1,0:T(8,128)(2,1)}, bf16[768,768]{1,0:T(8,128)(2,1)}, u32[]{:S(2)}, u32[]{:S(2)}) collective-permute-start(bf16[768,768]{1,0:T(8,128)(2,1)} %convolution_convert_fusion.9), channel_id=1, source_target_pairs={{0,1},{1,0},{2,3},{3,2},{4,5},{5,4},{6,7},{7,6},{8,9},{9,8},{10,11... | collective-permute-start | bytes 3538952 | tf_op jit(solution)/shard_map/ppermute | solution.py:260
  225.6 128.8 %collective-permute-start.9 = (bf16[768,768]{1,0:T(8,128)(2,1)}, bf16[768,768]{1,0:T(8,128)(2,1)}, u32[]{:S(2)}, u32[]{:S(2)}) collective-permute-start(bf16[768,768]{1,0:T(8,128)(2,1)} %convolution_convert_fusion.10), channel_id=1, source_target_pairs={{0,1},{1,0},{2,3},{3,2},{4,5},{5,4},{6,7},{7,6},{8,9},{9,8},{10,11... | collective-permute-start | bytes 3538952 | tf_op jit(solution)/shard_map/ppermute | solution.py:260
  226.3 3.5 copy-start.10
  229.6 67.0 %collective-permute-start.13 = (bf16[768,768]{1,0:T(8,128)(2,1)}, bf16[768,768]{1,0:T(8,128)(2,1)}, u32[]{:S(2)}, u32[]{:S(2)}) collective-permute-start(bf16[768,768]{1,0:T(8,128)(2,1)} %convolution_convert_fusion.7), channel_id=1, source_target_pairs={{0,1},{1,0},{2,3},{3,2},{4,5},{5,4},{6,7},{7,6},{8,9},{9,8},{10,11... | collective-permute-start | bytes 3538952 | tf_op jit(solution)/shard_map/ppermute | solution.py:260
  229.8 3.1 copy-start.30
  232.6 128.2 %collective-permute-start.12 = (bf16[768,768]{1,0:T(8,128)(2,1)}, bf16[768,768]{1,0:T(8,128)(2,1)}, u32[]{:S(2)}, u32[]{:S(2)}) collective-permute-start(bf16[768,768]{1,0:T(8,128)(2,1)} %convolution_convert_fusion.8), channel_id=1, source_target_pairs={{0,1},{1,0},{2,3},{3,2},{4,5},{5,4},{6,7},{7,6},{8,9},{9,8},{10,11... | collective-permute-start | bytes 3538952 | tf_op jit(solution)/shard_map/ppermute | solution.py:260
  240.1 24.9 %copy-start.3 = (f32[512,768]{1,0:T(8,128)S(1)}, f32[512,768]{1,0:T(8,128)}, u32[]{:S(2)}) copy-start(f32[512,768]{1,0:T(8,128)} %copy-done.2) | copy-start | bytes 4718596
  265.0 3.4 copy-start.4
  265.0 3.4 copy-start.14
  271.7 5.3 %copy-start.31 = (bf16[1088,768]{1,0:T(8,128)(2,1)S(1)}, bf16[1088,768]{1,0:T(8,128)(2,1)}, u32[]{:S(2)}) copy-start(bf16[1088,768]{1,0:T(8,128)(2,1)} %get-tuple-element.37) | copy-start | bytes 5013508
  278.4 3.2 copy-start.25
  285.7 24.8 %all-to-all-start.5 = ((bf16[4,192,512]{2,1,0:T(8,128)(2,1)}), bf16[4,192,512]{2,1,0:T(8,128)(2,1)}, u32[]{:S(2)}, u32[]{:S(2)}) async-start(bf16[4,192,512]{2,1,0:T(8,128)(2,1)} %bitcast.136), calls=%async_computation.5 | async-start | bytes 1572864 | tf_op jit(solution)/shard_map/all_to_all | solution.py:271
  289.9 6.7 %copy-start.12 = (bf16[1088,768]{1,0:T(8,128)(2,1)S(1)}, bf16[1088,768]{1,0:T(8,128)(2,1)}, u32[]{:S(2)}) copy-start(bf16[1088,768]{1,0:T(8,128)(2,1)} %copy-done.10) | copy-start | bytes 5013508
  289.9 6.7 %copy-start.28 = (bf16[1088,768]{1,0:T(8,128)(2,1)S(1)}, bf16[1088,768]{1,0:T(8,128)(2,1)}, u32[]{:S(2)}) copy-start(bf16[1088,768]{1,0:T(8,128)(2,1)} %get-tuple-element.39) | copy-start | bytes 5013508
  294.7 59.8 %collective-permute-start.11 = (bf16[768,768]{1,0:T(8,128)(2,1)}, bf16[768,768]{1,0:T(8,128)(2,1)S(1)}, u32[]{:S(2)}, u32[]{:S(2)}) collective-permute-start(bf16[768,768]{1,0:T(8,128)(2,1)} %add_convert_fusion.1), channel_id=1, source_target_pairs={{0,2},{1,3},{2,0},{3,1},{4,6},{5,7},{6,4},{7,5},{8,10},{9,11},{10,... | collective-permute-start | bytes 3538952 | tf_op jit(solution)/shard_map/ppermute | solution.py:260
  300.7 60.4 %collective-permute-start.14 = (bf16[768,768]{1,0:T(8,128)(2,1)}, bf16[768,768]{1,0:T(8,128)(2,1)}, u32[]{:S(2)}, u32[]{:S(2)}) collective-permute-start(bf16[768,768]{1,0:T(8,128)(2,1)} %add_convert_fusion), channel_id=1, source_target_pairs={{0,2},{1,3},{2,0},{3,1},{4,6},{5,7},{6,4},{7,5},{8,10},{9,11},{10,... | collective-permute-start | bytes 3538952 | tf_op jit(solution)/shard_map/ppermute | solution.py:260
  310.5 54.1 %all-to-all-start.2 = ((bf16[8,136,768]{2,1,0:T(8,128)(2,1)}), bf16[8,136,768]{2,1,0:T(8,128)(2,1)}, u32[]{:S(2)}, u32[]{:S(2)}) async-start(bf16[8,136,768]{2,1,0:T(8,128)(2,1)} %bitcast.10), calls=%async_computation.2 | async-start | bytes 3342336 | tf_op jit(solution)/shard_map/all_to_all | solution.py:265
  314.8 152.0 %all-reduce.6.cloned.1.call-start = ((), (), s32[]{:S(2)}) async-start(), calls=%async_computation.9 | async-start | bytes 4718592 | tf_op jit(solution)/shard_map/psum | solution.py:388
  315.1 28.0 %copy-start.16 = (bf16[768,192]{0,1:T(8,128)(2,1)S(1)}, bf16[768,192]{0,1:T(8,128)(2,1)}, u32[]{:S(2)}) copy-start(bf16[768,192]{0,1:T(8,128)(2,1)} %param.22) | copy-start | bytes 884740
  315.1 28.0 %copy-start.17 = (bf16[768,192]{0,1:T(8,128)(2,1)S(1)}, bf16[768,192]{0,1:T(8,128)(2,1)}, u32[]{:S(2)}) copy-start(bf16[768,192]{0,1:T(8,128)(2,1)} %param.23) | copy-start | bytes 884740
  343.2 7.4 %copy-start.34 = (bf16[2048,768]{1,0:T(8,128)(2,1)S(1)}, bf16[2048,768]{1,0:T(8,128)(2,1)}, u32[]{:S(2)}) copy-start(bf16[2048,768]{1,0:T(8,128)(2,1)} %get-tuple-element.24) | copy-start | bytes 9437188
  347.7 3.4 copy-start.36
  350.5 7.6 %collective-permute-start.7 = (bf16[512,768]{1,0:T(8,128)(2,1)}, bf16[512,768]{1,0:T(8,128)(2,1)}, u32[]{:S(2)}, u32[]{:S(2)}) collective-permute-start(bf16[512,768]{1,0:T(8,128)(2,1)} %get-tuple-element.47), channel_id=1, source_target_pairs={{0,1},{1,0},{2,3},{3,2},{4,5},{5,4},{6,7},{7,6},{8,9},{9,8},{10,11... | collective-permute-start | bytes 2359304 | tf_op jit(solution)/shard_map/ppermute | solution.py:260
  358.1 63.9 %collective-permute-start.6 = (bf16[512,768]{1,0:T(8,128)(2,1)}, bf16[512,768]{1,0:T(8,128)(2,1)}, u32[]{:S(2)}, u32[]{:S(2)}) collective-permute-start(bf16[512,768]{1,0:T(8,128)(2,1)} %get-tuple-element.46), channel_id=1, source_target_pairs={{0,1},{1,0},{2,3},{3,2},{4,5},{5,4},{6,7},{7,6},{8,9},{9,8},{10,11... | collective-permute-start | bytes 2359304 | tf_op jit(solution)/shard_map/ppermute | solution.py:260
  360.7 3.8 copy-start.5
  360.7 61.3 %collective-permute-start.8 = (bf16[512,768]{1,0:T(8,128)(2,1)}, bf16[512,768]{1,0:T(8,128)(2,1)}, u32[]{:S(2)}, u32[]{:S(2)}) collective-permute-start(bf16[512,768]{1,0:T(8,128)(2,1)} %fusion.43), channel_id=1, source_target_pairs={{0,2},{1,3},{2,0},{3,1},{4,6},{5,7},{6,4},{7,5},{8,10},{9,11},{10,... | collective-permute-start | bytes 2359304 | tf_op jit(solution)/shard_map/ppermute | solution.py:260
  364.6 3.8 copy-start.18
  466.8 3.5 copy-start.1
  (13 other events, 32.3 us)
Sparse Core Ops, SparseCore 0:
  9.6 20.1 all-gather.1
  271.9 40.1 reduce-scatter.1
  354.5 112.2 all-reduce.5

commit v2 on v1

--- a/solution.py
+++ b/solution.py
@@ -123,7 +123,7 @@
     lax.fori_loop(0, tiles, attend, 0)
 
 
-def bwd_kernel(len_ref, q_ref, kt_ref, kn_ref, vn_ref, lse_ref, att_ref, do_ref,
+def bwd_kernel(own_ref, len_ref, q_ref, kt_ref, kn_ref, vn_ref, lse_ref, att_ref, do_ref,
                out_ref, kh_ref, vh_ref, delta_ref, dq_ref, dk_ref, dv_ref):
     width, group = kt_ref.shape
     heads = width // HDIM
@@ -142,7 +142,7 @@
             vh_ref[head, rows, :] = jnp.where(mask, values, 0.0).astype(BF16)[:, 0:width]
             part = slice(head * HDIM, (head + 1) * HDIM)
             delta_ref[head:head + 1, rows] = jnp.sum(
-                do_ref[tile // per_block, part, spot].astype(F32) * att_ref[tile // per_block, part, spot].astype(F32),
+                do_ref[(tile // per_block) ^ own_ref[0], part, spot].astype(F32) * att_ref[tile // per_block, part, spot].astype(F32),
                 axis=0, keepdims=True)
         dq_ref[:, rows] = jnp.zeros((width, TILE), F32)
         return 0
@@ -159,7 +159,7 @@
             columns = pl.ds(pl.multiple_of(tile * TILE, TILE), TILE)
             spot = pl.ds(pl.multiple_of(lax.rem(tile, per_block) * TILE, TILE), TILE)
             queries = q_ref[:, columns]
-            grads = do_ref[tile // per_block, :, spot]
+            grads = do_ref[(tile // per_block) ^ own_ref[0], :, spot]
             for head in range(heads):
                 part = slice(head * HDIM, (head + 1) * HDIM)
                 scores = dot_nn(kh_ref[head, rows, :], queries)
@@ -205,7 +205,7 @@
     )(lengths, tokens, gain, wq, wk, wv)
 
 
-def attn_bwd(lengths, q, kt, kn, vn, lse, att, do):
+def attn_bwd(own, lengths, q, kt, kn, vn, lse, att, do):
     width, group = kt.shape
     lanes = kn.shape[1]
     heads = width // HDIM
@@ -213,14 +213,146 @@
     return pl.pallas_call(
         bwd_kernel,
         out_shape=S((3 * width, group), BF16),
-        in_specs=[SM] + [VM] * 7, out_specs=VM,
+        in_specs=[SM] * 2 + [VM] * 7, out_specs=VM,
         scratch_shapes=[pltpu.VMEM((heads, group, lanes), BF16), pltpu.VMEM((heads, group, width), BF16),
                         pltpu.VMEM((8, group), F32), pltpu.VMEM((width, group), F32),
                         pltpu.VMEM((width, TILE), F32), pltpu.VMEM((width, TILE), F32)],
         compiler_params=pltpu.CompilerParams(vmem_limit_bytes=LIMIT),
         cost_estimate=pl.CostEstimate(flops=16 * 10**9, bytes_accessed=10**7, transcendentals=4 * 10**6),
         name="attend_backward",
-    )(lengths, q, kt, kn, vn, lse, att, do)
+    )(own, lengths, q, kt, kn, vn, lse, att, do)
+
+
+MESH = pl.DeviceIdType.MESH
+
+
+def remote(source, target, send, recv, **device):
+    return pltpu.make_async_remote_copy(
+        src_ref=source, dst_ref=target, send_sem=send, recv_sem=recv,
+        device_id=device, device_id_type=MESH)
+
+
+def greet(n_wide, n_narrow):
+    me, here = lax.axis_index("wide"), lax.axis_index("narrow")
+    barrier = pltpu.get_barrier_semaphore()
+    for step in range(1, n_wide):
+        pl.semaphore_signal(barrier, inc=1, device_id={"wide": lax.rem(me + step, n_wide)}, device_id_type=MESH)
+    for bits in range(1, n_narrow):
+        pl.semaphore_signal(barrier, inc=1, device_id={"narrow": here ^ bits}, device_id_type=MESH)
+    pl.semaphore_wait(barrier, n_wide - 1 + n_narrow - 1)
+
+
+def tail_kernel(grad_ref, dense_ref, small_ref, grad_sum_ref, dense_sum_ref, small_sum_ref,
+                pair_in, chip_out, chip_in, half_in, half_sum, slab_in, small_in, small_mid, small_all,
+                pair_send, pair_recv, chip_send, chip_recv, half_send, half_recv, slab_send, slab_recv,
+                give_send, give_recv, last_send, last_recv, near_send, near_recv, all_send, all_recv):
+    chunks, half = dense_ref.shape[0], dense_ref.shape[1]
+    n_wide, n_narrow = 2 * half, small_ref.shape[0]
+    me, here = lax.axis_index("wide"), lax.axis_index("narrow")
+    core, chip = here ^ 1, here ^ 2
+    side, spot, partner = lax.rem(me, 2), me // 2, me ^ 1
+    greet(n_wide, n_narrow)
+
+    def ahead(step):
+        return lax.rem(spot + step, half)
+
+    def behind(step):
+        return lax.rem(spot + half - step, half)
+
+    halves = [remote(dense_ref.at[c, :, 1 - side], half_in.at[c], half_send.at[c], half_recv.at[c], wide=partner)
+              for c in range(chunks)]
+    pairs = [remote(grad_ref.at[here ^ (1 + 2 * i)], pair_in.at[i], pair_send.at[i], pair_recv.at[i], narrow=core)
+             for i in range(2)]
+    near = [remote(small_ref.at[here ^ bits], small_in.at[bits], near_send.at[bits], near_recv.at[bits],
+                   narrow=here ^ bits) for bits in range(1, n_narrow)]
+    slabs = [[remote(half_sum.at[c, ahead(step)], slab_in.at[c, step], slab_send.at[c, step], slab_recv.at[c, step],
+                     wide=2 * ahead(step) + side) for step in range(1, half)] for c in range(chunks)]
+    gives = [[remote(dense_sum_ref.at[c, spot, side], dense_sum_ref.at[c, spot, side], give_send.at[c, step],
+                     give_recv.at[c, step], wide=2 * ahead(step) + side) for step in range(1, half)]
+             for c in range(chunks)]
+    lasts = [remote(dense_sum_ref.at[c, :, side], dense_sum_ref.at[c, :, side], last_send.at[c], last_recv.at[c],
+                    wide=partner) for c in range(chunks)]
+    for one in near + pairs + halves:
+        one.start()
+
+    total = small_ref[here]
+    for bits in range(1, n_narrow):
+        near[bits - 1].wait_recv()
+        total = total + small_in[bits]
+    small_mid[...] = total
+    everyone = [remote(small_mid, small_all.at[step], all_send.at[step], all_recv.at[step],
+                       wide=lax.rem(me + step, n_wide)) for step in range(1, n_wide)]
+    for one in everyone:
+        one.start()
+
+    for one in pairs:
+        one.wait_recv()
+    chip_out[...] = (grad_ref[chip].astype(F32) + pair_in[1].astype(F32)).astype(BF16)
+    across = remote(chip_out, chip_in, chip_send, chip_recv, narrow=chip)
+    across.start()
+    grad_sum_ref[...] = grad_ref[here].astype(F32) + pair_in[0].astype(F32)
+
+    def to_owners(c):
+        halves[c].wait_recv()
+        half_sum[c] = (dense_ref[c, :, side].astype(F32) + half_in[c].astype(F32)).astype(BF16)
+        for one in slabs[c]:
+            one.start()
+
+    def to_peers(c):
+        part = half_sum[c, spot].astype(F32)
+        for step in range(1, half):
+            slabs[c][step - 1].wait_recv()
+            part = part + slab_in[c, step].astype(F32)
+        dense_sum_ref[c, spot, side] = part.astype(BF16)
+        for one in gives[c]:
+            one.start()
+
+    def to_partner(c):
+        for step in range(1, half):
+            source = behind(step)
+            remote(dense_sum_ref.at[c, source, side], dense_sum_ref.at[c, source, side], give_send.at[c, step],
+                   give_recv.at[c, step], wide=2 * source + side).wait_recv()
+        lasts[c].start()
+
+    for turn in range(chunks + 3):
+        for stage, act in ((0, to_owners), (1, to_peers), (3, to_partner)):
+            if 0 <= turn - stage < chunks:
+                act(turn - stage)
+
+    across.wait_recv()
+    grad_sum_ref[...] = grad_sum_ref[...] + chip_in[...].astype(F32)
+    total = small_mid[...]
+    for step in range(1, n_wide):
+        everyone[step - 1].wait_recv()
+        total = total + small_all[step]
+    small_sum_ref[...] = total
+    for c in range(chunks):
+        remote(dense_sum_ref.at[c, :, 1 - side], dense_sum_ref.at[c, :, 1 - side], last_send.at[c], last_recv.at[c],
+               wide=partner).wait_recv()
+    for one in pairs + near + halves + everyone + [across] + lasts + sum(slabs, []) + sum(gives, []):
+        one.wait_send()
+
+
+def tail_sums(grad, dense, small, n_wide):
+    n_narrow, half, rows = small.shape[0], n_wide // 2, dense.shape[0]
+    chunks = next(c for c in (3, 2, 1) if rows % (16 * n_wide * c) == 0 or c == 1)
+    dense = dense.reshape(chunks, half, 2, rows // (chunks * n_wide), -1)
+    S, V, D = jax.ShapeDtypeStruct, pltpu.VMEM, pltpu.SemaphoreType.DMA
+    one_side = (chunks, half) + dense.shape[3:]
+    sems = lambda *shape: [D(shape)] * 2
+    grad_sum, dense_sum, small_sum = pl.pallas_call(
+        tail_kernel,
+        out_shape=(S(grad.shape[1:], F32), S(dense.shape, BF16), S(small.shape[1:], F32)),
+        in_specs=[VM] * 3, out_specs=(VM,) * 3,
+        scratch_shapes=[V((2,) + grad.shape[1:], BF16), V(grad.shape[1:], BF16), V(grad.shape[1:], BF16),
+                        V(one_side, BF16), V(one_side, BF16), V(one_side, BF16),
+                        V(small.shape, F32), V(small.shape[1:], F32), V((n_wide,) + small.shape[1:], F32)]
+        + sems(2) + [D, D] + sems(chunks) + sems(chunks, half) * 2 + sems(chunks) + sems(n_narrow) + sems(n_wide),
+        compiler_params=pltpu.CompilerParams(collective_id=1, has_side_effects=True, vmem_limit_bytes=LIMIT),
+        cost_estimate=pl.CostEstimate(flops=10**6, bytes_accessed=10**8, transcendentals=0),
+        name="tail_sums",
+    )(grad, dense, small)
+    return grad_sum, dense_sum.reshape(rows, -1), small_sum
 
 
 def matmul(left, right):
@@ -298,10 +430,10 @@
 
     in_here, out_here = expert_in[0], expert_out[0]
     out_there = flip(out_here, 2)
-    in_there = flip(in_here, 2)
-    out_parts = [out_here, flip(out_here, 1), out_there, flip(out_there, 1)]
-    in_parts = [in_here, flip(in_here, 1), in_there, flip(in_there, 1)]
-    out_full = lax.all_gather(out_weight, "narrow", axis=0, tiled=True)
+    out_near = jnp.stack([out_weight, flip(out_weight, 1), flip(out_weight, 2), flip(out_weight, 3)])
+    out_full = jnp.concatenate([
+        lax.dynamic_index_in_dim(out_near, own_block ^ block, 0, keepdims=False) for block in range(narrow)
+    ])
 
     place = jnp.where(capacity_slots < capacity, routes * slots + capacity_slots, experts * slots)
     slot_ids = jnp.arange(experts * slots, dtype=jnp.int32)
@@ -316,6 +448,12 @@
     attn_in, att, lse, q_keep, kt_keep, kn_keep, vn_keep = attn_fwd(
         lengths, tokens, first_gain[None], query_t, jnp.pad(key_t, pad), jnp.pad(value_t, pad), narrow
     )
+    att, out_there, cot_rows, in_here = lax.optimization_barrier((att, out_there, cot_rows, in_here))
+    in_there = flip(in_here, 2)
+    out_parts = [out_here, flip(out_here, 1), out_there, flip(out_there, 1)]
+    backs = [times_transposed(cot_rows, w_out).astype(BF16) for w_out in out_parts]
+    *backs, in_there = lax.optimization_barrier((*backs, in_there))
+    in_parts = [in_here, flip(in_here, 1), in_there, flip(in_there, 1)]
     att_own = swap_narrow(att).reshape(narrow * width, block_rows)
     own_tokens = lax.dynamic_slice_in_dim(tokens, own_block * block_rows, block_rows, 0).astype(F32)
     hidden_one = own_tokens + inner_rows(att_own, out_full)
@@ -330,8 +468,7 @@
     gate = jnp.sum(probs * mine, axis=1, keepdims=True)
     grad_gate = jnp.zeros_like(gate)
     act_parts, pre_grads = [], []
-    for w_in, w_out in zip(in_parts, out_parts):
-        back = times_transposed(cot_rows, w_out).astype(BF16)
+    for w_in, back in zip(in_parts, backs):
         activated, slope = gelu_parts(matmul(rows, w_in))
         act_low = activated.astype(BF16)
         act_parts.append(act_low)
@@ -353,9 +490,10 @@
         one, three = flip(parts[1].astype(BF16), 1), flip(parts[3].astype(BF16), 1)
         keep = parts[0] + one.astype(F32)
         send = (parts[2] + three.astype(F32)).astype(BF16)
-        return keep + flip(send, 2).astype(F32)
-
-    out_grad, in_grad = sum_narrow(out_grads)[None], sum_narrow(in_grads)[None]
+        return keep, flip(send, 2)
+
+    out_keep, out_add = sum_narrow(out_grads)
+    in_keep, in_add = sum_narrow(in_grads)
 
     grad_moe_in = matmul(select, grad_home)
     mixed = hidden_one + matmul(select, result_home)
@@ -364,47 +502,50 @@
     grad_hidden = cotangent.astype(F32) + norm_back(grad_moe_in * second_gain, normed_two, root_two)
     grad_branch = grad_hidden.astype(BF16)
     grad_att = times_transposed(out_full, grad_branch).astype(BF16)
-    grad_heads = swap_narrow(grad_att.reshape(narrow, width, block_rows))
+    grad_att = grad_att.reshape(narrow, width, block_rows)
+
+    def heads_for(bits):
+        return lax.dynamic_index_in_dim(grad_att, own_block ^ bits, 0, keepdims=False)
+
+    grad_heads = jnp.stack([heads_for(0)] + [flip(heads_for(bits), bits) for bits in range(1, narrow)])
     out_part = matmul(att_own, grad_branch)
-    out_weight_grad = lax.psum(
-        lax.psum_scatter(out_part, "narrow", scatter_dimension=0, tiled=True), "wide"
-    )
-    small = lax.psum(
-        jnp.concatenate([router_part, second_part[:, None]], axis=1), ("wide", "narrow")
-    )
-
-    grad_qkv = attn_bwd(lengths, q_keep, kt_keep, kn_keep, vn_keep, lse, att, grad_heads)
+    part_keep, part_add = sum_narrow([
+        lax.dynamic_index_in_dim(out_part.reshape(narrow, width, model), own_block ^ bits, 0, keepdims=False)
+        for bits in range(narrow)
+    ])
+
+    grad_qkv = attn_bwd(own_block.reshape(1), lengths, q_keep, kt_keep, kn_keep, vn_keep, lse, att, grad_heads)
+    grad_qkv, out_add, in_add, part_add = lax.optimization_barrier((grad_qkv, out_add, in_add, part_add))
+    out_grad = (out_keep + out_add.astype(F32))[None]
+    in_grad = (in_keep + in_add.astype(F32))[None]
+    out_part = part_keep + part_add.astype(F32)
     qkv_t = jnp.concatenate([query_t, key_t, value_t], axis=0)
     grad_attn_in = inner_rows(grad_qkv, qkv_t).astype(BF16).reshape(narrow, block_rows, model)
 
-    def block_of(bits):
-        return lax.dynamic_index_in_dim(grad_attn_in, own_block ^ bits, 0, keepdims=False)
-
-    grad_rows_att = sum_narrow([block_of(bits).astype(F32) for bits in range(4)])
-    qkv_part = lax.dot_general(
-        attn_in, grad_qkv, (((0,), (1,)), ((), ())), preferred_element_type=F32
+    qkv_part = matmul(grad_qkv, attn_in)
+    first_part = jnp.sum(qkv_part * qkv_t.astype(F32), axis=0) / first_gain
+    small = jnp.concatenate([router_part, second_part[:, None], first_part[:, None]], axis=1).T
+    rows_small, lanes_small = -(-small.shape[0] // 8) * 8, -(-width // 128) * 128
+    small = small.reshape(-1, narrow, width).transpose(1, 0, 2)
+    small = jnp.pad(small, ((0, 0), (0, rows_small - small.shape[1]), (0, lanes_small - width)))
+    dense = jnp.concatenate([qkv_part.astype(BF16), out_part.astype(BF16)], axis=0)
+    grad_rows_att, dense, small = tail_sums(grad_attn_in, dense, small, experts)
+    query_grad, key_grad, value_grad, out_weight_grad = (
+        dense[i * width:(i + 1) * width].astype(F32) for i in range(4)
     )
-    first_part = jnp.sum(qkv_part * qkv_t.T.astype(F32), axis=1) / first_gain
-    qkv_grad = lax.psum(qkv_part, "wide")
-    first = lax.psum(first_part, ("wide", "narrow"))
     own_normed, own_root = norm_rows(own_tokens)
     token_grad = grad_hidden + norm_back(grad_rows_att * first_gain, own_normed, own_root)
 
-    def own_share(value):
-        size = value.shape[0] // narrow
-        return lax.dynamic_slice_in_dim(value, own_block * size, size, 0)
-
-    small = own_share(small)
     return (
         block_output,
         token_grad,
-        own_share(first),
-        small[:, experts],
-        qkv_grad[:, 0:width],
-        qkv_grad[:, width:2 * width],
-        qkv_grad[:, 2 * width:3 * width],
+        small[experts + 1, 0:width],
+        small[experts, 0:width],
+        query_grad.T,
+        key_grad.T,
+        value_grad.T,
         out_weight_grad,
-        small[:, 0:experts],
+        small[0:experts, 0:width].T,
         in_grad,
         out_grad,
     )

time: 483 us -> 407 us (0.84)
  waiting for transfers between devices: 166 us -> 105 us
  blocking collectives: 51.8 us -> 0 us
  Pallas kernels: 56.6 us -> 104 us
  other arithmetic: 20.5 us -> 40.2 us
  between operations: 14.7 us -> 1.76 us
  matrix products: 113 us -> 104 us
  local copies, waits for them, and re-layouts: 18.4 us -> 12.3 us
    psum x1 -> x0, blocking collectives: 51.8 us -> none  [local(): first = lax.psum(first_part, ('wide', 'narrow'))]
    pallas_call x0 -> x1, Pallas kernels: none -> 47.2 us  [tail_sums(): pl.pallas_call(tail_kernel, out_shape=(S(grad.shape[1:], F32), S(dense.sh...]
    psum x1 -> x0, waiting for transfers between devices: 38.3 us -> none  [local(): qkv_grad = lax.psum(qkv_part, 'wide')]
    all_to_all x2 -> x1, waiting for transfers between devices: 21.3 us -> 0.01 us  [swap_narrow(): lax.all_to_all(blocks, 'narrow', split_axis=0, concat_axis=0, tiled=True)]
    reduce_sum x0 -> x4, other arithmetic: none -> 14.4 us  [local(): jnp.sum(act_low.astype(F32) * back.astype(F32), axis=1, keepdims=True)]
    all_to_all x4, waiting for transfers between devices: 57.3 us -> 43.1 us  [swap_wide(): lax.all_to_all(rows.reshape(experts, -1, shape[1]), 'wide', split_axis=0,...]
    ppermute x15 -> x21, waiting for transfers between devices: 48 us -> 61.7 us  [flip(): return lax.ppermute(value, 'narrow', [(i, i ^ bit) for i in range(size)])]
    dot_general x10, matrix products: 35.8 us -> 26.1 us  [times_transposed(): lax.dot_general(left, right, (((1,), (1,)), ((), ())), preferred_element_...]
  transfers between devices with their start and end apart: 24 -> 26, of which waited for: 8 -> 9; matrix products, arithmetic and copies ran while one was open for 24% -> 29% of each run, Pallas kernels for 12% -> 26%
where the time goes in v2:
time: 407 us; the launch traced here: 401 us
  waiting for transfers between devices  105 us (26%)
  matrix products  104 us (26%)
  Pallas kernels  104 us (26%)
  other arithmetic  40.2 us (10%)
  starting transfers between devices  33.2 us (8%)
  local copies, waits for them, and re-layouts  12.3 us (3%)
    ppermute x21, waiting for transfers between devices, flip(): return lax.ppermute(value, 'narrow', [(i, i ^ bit) for i in range(size)])  61.7 us
    pallas_call x1, Pallas kernels, tail_sums(): pl.pallas_call(tail_kernel, out_shape=(S(grad.shape[1:], F32), S(dense.sh...  47.2 us
    dot_general x13, matrix products, inner_rows(): lax.dot_general(left, right, (((0,), (0,)), ((), ())), preferred_element_...  44.7 us
    all_to_all x4, waiting for transfers between devices, swap_wide(): lax.all_to_all(rows.reshape(experts, -1, shape[1]), 'wide', split_axis=0,...  43.1 us
    dot_general x13, matrix products, matmul(): return jnp.dot(left, right, preferred_element_type=F32)  33.6 us
    pallas_call x1, Pallas kernels, attn_fwd(): pl.pallas_call(fwd_kernel, out_shape=(S((group, model), BF16), S((blocks,...  28.5 us
    pallas_call x1, Pallas kernels, attn_bwd(): pl.pallas_call(bwd_kernel, out_shape=S((3 * width, group), BF16), in_spec...  28.3 us
    dot_general x10, matrix products, times_transposed(): lax.dot_general(left, right, (((1,), (1,)), ((), ())), preferred_element_...  26.1 us
  transfers between devices with their start and end apart: 26, of which 9 were waited for; matrix products, arithmetic and copies ran while one was open for 29% of the time, Pallas kernels for 26%

profile of v2, /device:TPU:0, one launch (start us, length us, event | category | flops | bytes accessed | tf_op | source)
XLA Modules:
  0.0 400.7 jit_solution(7611102619339474985)
XLA Ops:
  1.4 3.6 convolution_convert_fusion.1
  5.0 7.4 %all-to-all-start = ((bf16[8,136,768]{2,1,0:T(8,128)(2,1)}), bf16[8,136,768]{2,1,0:T(8,128)(2,1)S(1)}, u32[]{:S(2)}, u32[]{:S(2)}) async-start(bf16[8,136,768]{2,1,0:T(8,128)(2,1)} %bitcast.6), calls=%async_computation | async-start | bytes 3342336 | tf_op jit(solution)/shard_map/all_to_all | solution.py:397
  16.0 28.5 %attend_forward.1 = (bf16[2048,768]{1,0:T(8,128)(2,1)}, bf16[4,192,512]{2,1,0:T(8,128)(2,1)}, f32[8,2048]{1,0:T(8,128)}, bf16[256,2048]{1,0:T(8,128)(2,1)}, bf16...) custom-call(s32[1,8]{1,0:T(1,128)} %len_ref.3, bf16[2048,768]{1,0:T(8,128)(2,1)} %tok_ref.1, ...), custom_call_target="tpu_custom_call" | custom-call | flops 8000000000 | bytes 10000000 | tf_op jit(solution)/shard_map/attend_forward/pallas_call | solution.py:195
  44.6 6.9 %all-to-all-done = bf16[8,136,768]{2,1,0:T(8,128)(2,1)S(1)} async-done(((bf16[8,136,768]{2,1,0:T(8,128)(2,1)}), bf16[8,136,768]{2,1,0:T(8,128)(2,1)S(1)}, u32[]{:S(2)}, u32[]{:S(2)}) %all-to-all-start) | async-done | bytes 1671200 | tf_op jit(solution)/shard_map/all_to_all | solution.py:397
  51.5 3.5 all-to-all-start.1
  57.2 16.2 %collective-permute-done.2 = bf16[192,768]{1,0:T(8,128)(2,1)S(1)} collective-permute-done((bf16[192,768]{1,0:T(8,128)(2,1)S(1)}, bf16[192,768]{1,0:T(8,128)(2,1)S(1)}, u32[]{:S(2)}, u32[]{:S(2)}) %collective-permute-start.2) | collective-permute-done | bytes 294944 | tf_op jit(solution)/shard_map/ppermute | solution.py:392
  73.4 5.5 %collective-permute-done.3 = bf16[192,768]{1,0:T(8,128)(2,1)} collective-permute-done((bf16[192,768]{1,0:T(8,128)(2,1)S(1)}, bf16[192,768]{1,0:T(8,128)(2,1)}, u32[]{:S(2)}, u32[]{:S(2)}) %collective-permute-start.3) | collective-permute-done | bytes 294944 | tf_op jit(solution)/shard_map/ppermute | solution.py:392
  80.8 2.7 fusion.73
  86.6 3.9 all-to-all-start.2
  95.1 4.0 convolution_convert_fusion.4
  99.1 2.8 convolution_convert_fusion.6
  101.9 4.0 %convolution_convert_fusion.5 = bf16[1088,768]{1,0:T(8,128)(2,1)} fusion(bf16[1088,768]{1,0:T(8,128)(2,1)S(1)} %bitcast.153, bf16[768,768]{1,0:T(8,128)(2,1)} %collective-permute-done.5), kind=kOutput, calls=%fused_computation.27 | convolution fusion | flops 1284292608 | bytes 4521984 | tf_op jit(solution)/shard_map/dot_general | solution.py:367
  108.6 14.3 %collective-permute-done.7 = bf16[768,768]{1,0:T(8,128)(2,1)} collective-permute-done((bf16[768,768]{1,0:T(8,128)(2,1)}, bf16[768,768]{1,0:T(8,128)(2,1)}, u32[]{:S(2)}, u32[]{:S(2)}) %collective-permute-start.7) | collective-permute-done | bytes 1179680 | tf_op jit(solution)/shard_map/ppermute | solution.py:392
  122.9 7.3 %all-to-all-done.2 = bf16[8,136,768]{2,1,0:T(8,128)(2,1)S(1)} async-done(((bf16[8,136,768]{2,1,0:T(8,128)(2,1)}), bf16[8,136,768]{2,1,0:T(8,128)(2,1)S(1)}, u32[]{:S(2)}, u32[]{:S(2)}) %all-to-all-start.2) | async-done | bytes 1671200 | tf_op jit(solution)/shard_map/all_to_all | solution.py:397
  130.2 2.7 fusion.77
  135.7 2.9 fusion.12
  138.7 3.4 fusion.76
  142.1 3.7 fusion.9
  145.8 4.1 %fusion.6 = (f32[1088]{0:T(1024)S(1)}, bf16[1088,768]{1,0:T(8,128)(2,1)}, bf16[1088,768]{1,0:T(8,128)(2,1)S(1)}) fusion(bf16[1088,768]{1,0:T(8,128)(2,1)S(1)} %copy-done.23, f32[1088,768]{1,0:T(8,128)S(1)} %fusion.75, f32[1088]{0:T(1024)S(1)} %multiply_reduce_fusion.6), kind=kLoop, calls=%fused_computation.29 | loop fusion | flops 14203840 | bytes 8364544 | tf_op jit(solution)/shard_map/reduce_sum | solution.py:475
  149.9 3.4 fusion.78
  153.3 3.7 fusion.15
  157.8 2.8 fusion.81
  160.5 2.8 convolution_convert_fusion.9
  164.9 2.8 fusion.82
  167.7 4.1 %fusion.5 = bf16[1088,768]{1,0:T(8,128)(2,1)} fusion(f32[1088,768]{1,0:T(8,128)S(1)} %fusion.82, f32[1088,768]{1,0:T(8,128)S(1)} %fusion.81, f32[1088,768]{1,0:T(8,128)S(1)} %convolution_add_fusion.1, bf16[1088,768]{1,0:T(8,128)(2,1)S(1)} %get-tuple-element.70, bf16[768,768]{1,0:T(8,128)(2,1)} %collective-permute-done.4), kind=kOutput, calls=%fused_computation.21 | convolution fusion | flops 1286799360 | bytes 14548992 | tf_op jit(solution)/shard_map/dot_general | solution.py:367
  171.7 4.5 %all-to-all-start.4 = ((bf16[8,136,768]{2,1,0:T(8,128)(2,1)}), bf16[8,136,768]{2,1,0:T(8,128)(2,1)}, u32[]{:S(2)}, u32[]{:S(2)}) async-start(bf16[8,136,768]{2,1,0:T(8,128)(2,1)} %bitcast.22), calls=%async_computation.4 | async-start | bytes 3342336 | tf_op jit(solution)/shard_map/all_to_all | solution.py:397
  176.3 5.0 %convolution_convert_fusion.10 = bf16[768,768]{1,0:T(8,128)(2,1)} fusion(bf16[1088,768]{1,0:T(8,128)(2,1)} %get-tuple-element.69, bf16[1088,768]{1,0:T(8,128)(2,1)} %bitcast.155, f32[1088]{0:T(1024)S(1)} %multiply_reduce_fusion.6), kind=kOutput, calls=%fused_computation.95 | convolution fusion | flops 1286553600 | bytes 4526336 | tf_op jit(solution)/shard_map/dot_general | solution.py:363
  185.0 2.9 convolution_convert_fusion.7
  187.9 2.9 convolution_add_fusion.3
  193.5 2.8 convolution_convert_fusion.8
  196.8 3.2 fusion.84
  200.0 3.6 fusion.69
  203.6 11.3 %all-to-all-done.4 = bf16[8,136,768]{2,1,0:T(8,128)(2,1)} async-done(((bf16[8,136,768]{2,1,0:T(8,128)(2,1)}), bf16[8,136,768]{2,1,0:T(8,128)(2,1)}, u32[]{:S(2)}, u32[]{:S(2)}) %all-to-all-start.4) | async-done | bytes 1671200 | tf_op jit(solution)/shard_map/all_to_all | solution.py:397
  214.9 4.3 %all-to-all-start.3 = ((bf16[8,136,768]{2,1,0:T(8,128)(2,1)}), bf16[8,136,768]{2,1,0:T(8,128)(2,1)}, u32[]{:S(2)}, u32[]{:S(2)}) async-start(bf16[8,136,768]{2,1,0:T(8,128)(2,1)} %bitcast.20), calls=%async_computation.3 | async-start | bytes 3342336 | tf_op jit(solution)/shard_map/all_to_all | solution.py:397
  220.7 4.1 %add_convert_fusion = bf16[768,768]{1,0:T(8,128)(2,1)} fusion(bf16[768,768]{1,0:T(8,128)(2,1)} %collective-permute-done.14, bf16[1088,768]{1,0:T(8,128)(2,1)S(1)} %bitcast.147, bf16[1088,768]{1,0:T(8,128)(2,1)S(1)} %copy-done.17), kind=kOutput, calls=%fused_computation.71 | convolution fusion | flops 1285226496 | bytes 5701632 | tf_op jit(solution)/shard_map/dot_general | solution.py:363
  224.8 4.4 %add_convert_fusion.1 = bf16[768,768]{1,0:T(8,128)(2,1)} fusion(bf16[768,768]{1,0:T(8,128)(2,1)} %collective-permute-done.12, bf16[1088,768]{1,0:T(8,128)(2,1)S(1)} %get-tuple-element.67, bf16[1088,768]{1,0:T(8,128)(2,1)S(1)} %bitcast.158, f32[1088]{0:T(1024)S(1)} %multiply_reduce_fusion.6), kind=kOutput, calls=%fused_computation.72 | convolution fusion | flops 1287733248 | bytes 5705984 | tf_op jit(solution)/shard_map/dot_general | solution.py:363
  229.2 3.3 multiply_reduce_fusion.1
  240.3 17.6 %all-to-all-done.3 = bf16[8,136,768]{2,1,0:T(8,128)(2,1)} async-done(((bf16[8,136,768]{2,1,0:T(8,128)(2,1)}), bf16[8,136,768]{2,1,0:T(8,128)(2,1)}, u32[]{:S(2)}, u32[]{:S(2)}) %all-to-all-start.3) | async-done | bytes 1671200 | tf_op jit(solution)/shard_map/all_to_all | solution.py:397
  258.0 3.8 add_convert_fusion.2
  268.1 28.3 %attend_backward.1 = bf16[576,2048]{1,0:T(8,128)(2,1)} custom-call(s32[1]{0:T(128)} %bitcast.24.own_ref, s32[1,8]{1,0:T(1,128)} %len_ref.3, bf16[256,2048]{1,0:T(8,128)(2,1)} %get-tuple-element.44.q_ref, bf16[192,2048]{1,0:T(8,128)(2,1)} %get-tuple-element.45.kt_ref, bf16[2048,256]{1,0:T(8,128)(2,1)} %get-tuple-element.46.kn_ref, ...), custom_call_target="tpu_custom_call" | custom-call | flops 16000000000 | bytes 10000000 | tf_op jit(solution)/shard_map/attend_backward/pallas_call | solution.py:213
  296.4 19.8 %collective-permute-done.13 = bf16[768,768]{1,0:T(8,128)(2,1)} collective-permute-done((bf16[768,768]{1,0:T(8,128)(2,1)}, bf16[768,768]{1,0:T(8,128)(2,1)}, u32[]{:S(2)}, u32[]{:S(2)}) %collective-permute-start.13) | collective-permute-done | bytes 1179680 | tf_op jit(solution)/shard_map/ppermute | solution.py:392
  316.2 5.8 %collective-permute-done.17 = bf16[192,768]{1,0:T(8,128)(2,1)S(1)} collective-permute-done((bf16[192,768]{1,0:T(8,128)(2,1)}, bf16[192,768]{1,0:T(8,128)(2,1)S(1)}, u32[]{:S(2)}, u32[]{:S(2)}) %collective-permute-start.17) | collective-permute-done | bytes 294944 | tf_op jit(solution)/shard_map/ppermute | solution.py:392
  322.0 5.6 %multiply_reduce_fusion = (f32[768]{0:T(1024)S(1)}, bf16[576,768]{1,0:T(8,128)(2,1)}) fusion(bf16[192,768]{1,0:T(8,128)(2,1)S(1)} %bitcast.169, bf16[192,768]{1,0:T(8,128)(2,1)S(1)} %bitcast.166, bf16[192,768]{1,0:T(8,128)(2,1)} %bitcast.190, bf16[576,2048]{1,0:T(8,128)(2,1)} %attend_backward.1, bf16[2048,768]{1,0:T(8,128)(2,1)} %get-tuple-element.50), kind=kOutput, calls=%fused_computation.80 | convolution fusion | flops 1815919872 | bytes 7277568 | tf_op jit(solution)/shard_map/dot_general | solution.py:359
  328.4 6.0 %convolution_convert_fusion.2 = bf16[2048,768]{1,0:T(8,128)(2,1)} fusion(bf16[576,2048]{1,0:T(8,128)(2,1)} %attend_backward.1, bf16[192,768]{1,0:T(8,128)(2,1)S(1)} %bitcast.170, bf16[192,768]{1,0:T(8,128)(2,1)S(1)} %bitcast.167, bf16[192,768]{1,0:T(8,128)(2,1)} %bitcast.191), kind=kOutput, calls=%fused_computation.24 | convolution fusion | flops 1816166400 | bytes 6389760 | tf_op jit(solution)/shard_map/dot_general | solution.py:363
  336.9 47.2 %tail_sums.1 = (f32[512,768]{1,0:T(8,128)}, bf16[3,4,2,32,768]{4,3,2,1,0:T(8,128)(2,1)}, f32[16,256]{1,0:T(8,128)}) custom-call(bf16[4,512,768]{2,1,0:T(8,128)(2,1)} %bitcast.150, bf16[3,4,2,32,768]{4,3,2,1,0:T(8,128)(2,1)} %bitcast.148, f32[4,16,256]{2,1,0:T(8,128)} %pad.13.small_ref), custom_call_target="tpu_custom_call" | custom-call | flops 1000000 | bytes 100000000 | tf_op jit(solution)/shard_map/tail_sums/pallas_call | solution.py:343
  390.7 3.0 fusion.42
  393.7 3.5 add_bitcast_fusion
  397.2 3.0 add_bitcast_fusion.1
  (214 shorter events, 56.1 us)
Async XLA Ops:
  0.6 132.3 %copy-start = (bf16[768,8]{0,1:T(8,128)(2,1)S(1)}, bf16[768,8]{0,1:T(8,128)(2,1)}, u32[]{:S(2)}) copy-start(bf16[768,8]{0,1:T(8,128)(2,1)} %param.25) | copy-start | bytes 36868
  1.4 227.8 %copy-start.53 = (s32[512,1]{0,1:T(1,128)}, s32[512,1]{0,1:T(1,128)S(1)}, u32[]{:S(2)}) copy-start(s32[512,1]{0,1:T(1,128)S(1)} %get-tuple-element.92) | copy-start | bytes 6148
  1.4 227.8 %copy-start.55 = (s32[512,1]{0,1:T(1,128)}, s32[512,1]{0,1:T(1,128)S(1)}, u32[]{:S(2)}) copy-start(s32[512,1]{0,1:T(1,128)S(1)} %get-tuple-element.93) | copy-start | bytes 6148
  5.0 8.9 %copy-start.33 = (bf16[768,192]{0,1:T(8,128)(2,1)S(1)}, bf16[768,192]{0,1:T(8,128)(2,1)}, u32[]{:S(2)}) copy-start(bf16[768,192]{0,1:T(8,128)(2,1)} %param.22) | copy-start | bytes 884740
  5.0 9.7 %copy-start.35 = (bf16[768,192]{0,1:T(8,128)(2,1)S(1)}, bf16[768,192]{0,1:T(8,128)(2,1)}, u32[]{:S(2)}) copy-start(bf16[768,192]{0,1:T(8,128)(2,1)} %param.23) | copy-start | bytes 884740
  5.0 10.5 %copy-start.47 = (f32[768]{0:T(1024)S(1)}, f32[768]{0:T(1024)}, u32[]{:S(2)}) copy-start(f32[768]{0:T(1024)} %param.19) | copy-start | bytes 9220
  5.0 46.5 %all-to-all-start = ((bf16[8,136,768]{2,1,0:T(8,128)(2,1)}), bf16[8,136,768]{2,1,0:T(8,128)(2,1)S(1)}, u32[]{:S(2)}, u32[]{:S(2)}) async-start(bf16[8,136,768]{2,1,0:T(8,128)(2,1)} %bitcast.6), calls=%async_computation | async-start | bytes 3342336 | tf_op jit(solution)/shard_map/all_to_all | solution.py:397
  12.4 32.2 %collective-permute-start = (bf16[768,768]{1,0:T(8,128)(2,1)}, bf16[768,768]{1,0:T(8,128)(2,1)S(1)}, u32[]{:S(2)}, u32[]{:S(2)}) collective-permute-start(bf16[768,768]{1,0:T(8,128)(2,1)} %bitcast.187), channel_id=1, source_target_pairs={{0,2},{1,3},{2,0},{3,1},{4,6},{5,7},{6,4},{7,5},{8,10},{9,11},{10,... | collective-permute-start | bytes 3538952 | tf_op jit(solution)/shard_map/ppermute | solution.py:392
  16.0 39.0 %copy-start.32 = (bf16[192,768]{1,0:T(8,128)(2,1)S(1)}, bf16[192,768]{1,0:T(8,128)(2,1)}, u32[]{:S(2)}) copy-start(bf16[192,768]{1,0:T(8,128)(2,1)} %param.24) | copy-start | bytes 884740
  44.6 6.9 %copy-start.27 = (bf16[768,768]{1,0:T(8,128)(2,1)}, bf16[768,768]{1,0:T(8,128)(2,1)S(1)}, u32[]{:S(2)}) copy-start(bf16[768,768]{1,0:T(8,128)(2,1)S(1)} %collective-permute-done) | copy-start | bytes 3538948
  51.5 54.5 %copy-start.13 = (bf16[8,136,768]{2,1,0:T(8,128)(2,1)}, bf16[8,136,768]{2,1,0:T(8,128)(2,1)S(1)}, u32[]{:S(2)}) copy-start(bf16[8,136,768]{2,1,0:T(8,128)(2,1)S(1)} %all-to-all-done) | copy-start | bytes 5013508
  51.5 29.3 %all-to-all-start.1 = ((bf16[4,192,512]{2,1,0:T(8,128)(2,1)}), bf16[4,192,512]{2,1,0:T(8,128)(2,1)S(1)}, u32[]{:S(2)}, u32[]{:S(2)}) async-start(bf16[4,192,512]{2,1,0:T(8,128)(2,1)} %get-tuple-element.35.att_ref), calls=%async_computation.1 | async-start | bytes 1572864 | tf_op jit(solution)/shard_map/all_to_all | solution.py:403
  55.0 2.2 collective-permute-start.1
  55.5 17.9 %collective-permute-start.2 = (bf16[192,768]{1,0:T(8,128)(2,1)S(1)}, bf16[192,768]{1,0:T(8,128)(2,1)S(1)}, u32[]{:S(2)}, u32[]{:S(2)}) collective-permute-start(bf16[192,768]{1,0:T(8,128)(2,1)S(1)} %copy-done.32), channel_id=1, source_target_pairs={{0,2},{1,3},{2,0},{3,1},{4,6},{5,7},{6,4},{7,5},{8,10},{9,11},{10,... | collective-permute-start | bytes 884744 | tf_op jit(solution)/shard_map/ppermute | solution.py:392
  57.1 21.7 %collective-permute-start.3 = (bf16[192,768]{1,0:T(8,128)(2,1)S(1)}, bf16[192,768]{1,0:T(8,128)(2,1)}, u32[]{:S(2)}, u32[]{:S(2)}) collective-permute-start(bf16[192,768]{1,0:T(8,128)(2,1)S(1)} %copy-done.32), channel_id=1, source_target_pairs={{0,3},{1,2},{2,1},{3,0},{4,7},{5,6},{6,5},{7,4},{8,11},{9,10},{10,... | collective-permute-start | bytes 884744 | tf_op jit(solution)/shard_map/ppermute | solution.py:392
  86.6 43.6 %all-to-all-start.2 = ((bf16[8,136,768]{2,1,0:T(8,128)(2,1)}), bf16[8,136,768]{2,1,0:T(8,128)(2,1)S(1)}, u32[]{:S(2)}, u32[]{:S(2)}) async-start(bf16[8,136,768]{2,1,0:T(8,128)(2,1)} %bitcast.159), calls=%async_computation.2 | async-start | bytes 3342336 | tf_op jit(solution)/shard_map/all_to_all | solution.py:397
  90.5 11.4 %collective-permute-start.5 = (bf16[768,768]{1,0:T(8,128)(2,1)}, bf16[768,768]{1,0:T(8,128)(2,1)}, u32[]{:S(2)}, u32[]{:S(2)}) collective-permute-start(bf16[768,768]{1,0:T(8,128)(2,1)} %bitcast.188), channel_id=1, source_target_pairs={{0,1},{1,0},{2,3},{3,2},{4,5},{5,4},{6,7},{7,6},{8,9},{9,8},{10,11... | collective-permute-start | bytes 3538952 | tf_op jit(solution)/shard_map/ppermute | solution.py:392
  92.1 7.0 %copy-start.48 = (f32[512]{0:T(512)}, f32[512]{0:T(512)S(1)}, u32[]{:S(2)}) copy-start(f32[512]{0:T(512)S(1)} %broadcast_multiply_fusion.2) | copy-start | bytes 6148
  94.2 11.7 %collective-permute-start.6 = (bf16[768,768]{1,0:T(8,128)(2,1)}, bf16[768,768]{1,0:T(8,128)(2,1)S(1)}, u32[]{:S(2)}, u32[]{:S(2)}) collective-permute-start(bf16[768,768]{1,0:T(8,128)(2,1)} %copy-done.27), channel_id=1, source_target_pairs={{0,1},{1,0},{2,3},{3,2},{4,5},{5,4},{6,7},{7,6},{8,9},{9,8},{10,11... | collective-permute-start | bytes 3538952 | tf_op jit(solution)/shard_map/ppermute | solution.py:392
  94.5 28.4 %collective-permute-start.7 = (bf16[768,768]{1,0:T(8,128)(2,1)}, bf16[768,768]{1,0:T(8,128)(2,1)}, u32[]{:S(2)}, u32[]{:S(2)}) collective-permute-start(bf16[768,768]{1,0:T(8,128)(2,1)} %bitcast.183), channel_id=1, source_target_pairs={{0,2},{1,3},{2,0},{3,1},{4,6},{5,7},{6,4},{7,5},{8,10},{9,11},{10,... | collective-permute-start | bytes 3538952 | tf_op jit(solution)/shard_map/ppermute | solution.py:392
  95.1 43.5 %collective-permute-start.4 = (bf16[768,768]{1,0:T(8,128)(2,1)}, bf16[768,768]{1,0:T(8,128)(2,1)}, u32[]{:S(2)}, u32[]{:S(2)}) collective-permute-start(bf16[768,768]{1,0:T(8,128)(2,1)} %bitcast.184), channel_id=1, source_target_pairs={{0,1},{1,0},{2,3},{3,2},{4,5},{5,4},{6,7},{7,6},{8,9},{9,8},{10,11... | collective-permute-start | bytes 3538952 | tf_op jit(solution)/shard_map/ppermute | solution.py:392
  122.9 27.0 %collective-permute-start.8 = (bf16[768,768]{1,0:T(8,128)(2,1)}, bf16[768,768]{1,0:T(8,128)(2,1)}, u32[]{:S(2)}, u32[]{:S(2)}) collective-permute-start(bf16[768,768]{1,0:T(8,128)(2,1)} %collective-permute-done.7), channel_id=1, source_target_pairs={{0,1},{1,0},{2,3},{3,2},{4,5},{5,4},{6,7},{7,6},{8,9},{9,8},{10,11... | collective-permute-start | bytes 3538952 | tf_op jit(solution)/shard_map/ppermute | solution.py:392
  138.6 19.1 %copy-start.16 = (bf16[1088,768]{1,0:T(8,128)(2,1)}, bf16[1088,768]{1,0:T(8,128)(2,1)S(1)}, u32[]{:S(2)}) copy-start(bf16[1088,768]{1,0:T(8,128)(2,1)S(1)} %get-tuple-element.72) | copy-start | bytes 5013508
  145.8 21.8 %copy-start.3 = (bf16[1088,768]{1,0:T(8,128)(2,1)}, bf16[1088,768]{1,0:T(8,128)(2,1)S(1)}, u32[]{:S(2)}) copy-start(bf16[1088,768]{1,0:T(8,128)(2,1)S(1)} %get-tuple-element.70) | copy-start | bytes 5013508
  149.9 13.4 %copy-start.19 = (bf16[1088,768]{1,0:T(8,128)(2,1)}, bf16[1088,768]{1,0:T(8,128)(2,1)S(1)}, u32[]{:S(2)}) copy-start(bf16[1088,768]{1,0:T(8,128)(2,1)S(1)} %get-tuple-element.71) | copy-start | bytes 5013508
  171.7 43.2 %all-to-all-start.4 = ((bf16[8,136,768]{2,1,0:T(8,128)(2,1)}), bf16[8,136,768]{2,1,0:T(8,128)(2,1)}, u32[]{:S(2)}, u32[]{:S(2)}) async-start(bf16[8,136,768]{2,1,0:T(8,128)(2,1)} %bitcast.22), calls=%async_computation.4 | async-start | bytes 3342336 | tf_op jit(solution)/shard_map/all_to_all | solution.py:397
  176.2 44.0 %collective-permute-start.14 = (bf16[768,768]{1,0:T(8,128)(2,1)}, bf16[768,768]{1,0:T(8,128)(2,1)}, u32[]{:S(2)}, u32[]{:S(2)}) collective-permute-start(bf16[768,768]{1,0:T(8,128)(2,1)} %convolution_convert_fusion.9), channel_id=1, source_target_pairs={{0,1},{1,0},{2,3},{3,2},{4,5},{5,4},{6,7},{7,6},{8,9},{9,8},{10,11... | collective-permute-start | bytes 3538952 | tf_op jit(solution)/shard_map/ppermute | solution.py:392
  196.4 28.4 %collective-permute-start.12 = (bf16[768,768]{1,0:T(8,128)(2,1)}, bf16[768,768]{1,0:T(8,128)(2,1)}, u32[]{:S(2)}, u32[]{:S(2)}) collective-permute-start(bf16[768,768]{1,0:T(8,128)(2,1)} %convolution_convert_fusion.10), channel_id=1, source_target_pairs={{0,1},{1,0},{2,3},{3,2},{4,5},{5,4},{6,7},{7,6},{8,9},{9,8},{10,11... | collective-permute-start | bytes 3538952 | tf_op jit(solution)/shard_map/ppermute | solution.py:392
  214.9 43.0 %all-to-all-start.3 = ((bf16[8,136,768]{2,1,0:T(8,128)(2,1)}), bf16[8,136,768]{2,1,0:T(8,128)(2,1)}, u32[]{:S(2)}, u32[]{:S(2)}) async-start(bf16[8,136,768]{2,1,0:T(8,128)(2,1)} %bitcast.20), calls=%async_computation.3 | async-start | bytes 3342336 | tf_op jit(solution)/shard_map/all_to_all | solution.py:397
  220.2 173.5 %collective-permute-start.20 = (bf16[768,768]{1,0:T(8,128)(2,1)}, bf16[768,768]{1,0:T(8,128)(2,1)}, u32[]{:S(2)}, u32[]{:S(2)}) collective-permute-start(bf16[768,768]{1,0:T(8,128)(2,1)} %convolution_convert_fusion.7), channel_id=1, source_target_pairs={{0,1},{1,0},{2,3},{3,2},{4,5},{5,4},{6,7},{7,6},{8,9},{9,8},{10,11... | collective-permute-start | bytes 3538952 | tf_op jit(solution)/shard_map/ppermute | solution.py:392
  236.7 21.2 %copy-start.7 = (f32[512,768]{1,0:T(8,128)S(1)}, f32[512,768]{1,0:T(8,128)}, u32[]{:S(2)}) copy-start(f32[512,768]{1,0:T(8,128)} %copy-done.5) | copy-start | bytes 4718596
  236.7 21.2 %copy-start.54 = (s32[512,1]{0,1:T(1,128)S(1)}, s32[512,1]{0,1:T(1,128)}, u32[]{:S(2)}) copy-start(s32[512,1]{0,1:T(1,128)} %copy-done.53) | copy-start | bytes 6148
  236.7 21.2 %copy-start.56 = (s32[512,1]{0,1:T(1,128)S(1)}, s32[512,1]{0,1:T(1,128)}, u32[]{:S(2)}) copy-start(s32[512,1]{0,1:T(1,128)} %copy-done.55) | copy-start | bytes 6148
  236.8 29.1 %collective-permute-start.16 = (bf16[192,768]{1,0:T(8,128)(2,1)}, bf16[192,768]{1,0:T(8,128)(2,1)}, u32[]{:S(2)}, u32[]{:S(2)}) collective-permute-start(bf16[192,768]{1,0:T(8,128)(2,1)} %get-tuple-element.75), channel_id=1, source_target_pairs={{0,1},{1,0},{2,3},{3,2},{4,5},{5,4},{6,7},{7,6},{8,9},{9,8},{10,11... | collective-permute-start | bytes 884744 | tf_op jit(solution)/shard_map/ppermute | solution.py:392
  238.5 23.3 %collective-permute-start.9 = (bf16[192,512]{1,0:T(8,128)(2,1)}, bf16[192,512]{1,0:T(8,128)(2,1)S(1)}, u32[]{:S(2)}, u32[]{:S(2)}) collective-permute-start(bf16[192,512]{1,0:T(8,128)(2,1)} %get-tuple-element.89), channel_id=1, source_target_pairs={{0,1},{1,0},{2,3},{3,2},{4,5},{5,4},{6,7},{7,6},{8,9},{9,8},{10,11... | collective-permute-start | bytes 589832 | tf_op jit(solution)/shard_map/ppermute | solution.py:392
  238.9 22.8 %collective-permute-start.10 = (bf16[192,512]{1,0:T(8,128)(2,1)}, bf16[192,512]{1,0:T(8,128)(2,1)}, u32[]{:S(2)}, u32[]{:S(2)}) collective-permute-start(bf16[192,512]{1,0:T(8,128)(2,1)} %get-tuple-element.88), channel_id=1, source_target_pairs={{0,2},{1,3},{2,0},{3,1},{4,6},{5,7},{6,4},{7,5},{8,10},{9,11},{10,... | collective-permute-start | bytes 589832 | tf_op jit(solution)/shard_map/ppermute | solution.py:392
  239.2 22.9 %collective-permute-start.11 = (bf16[192,512]{1,0:T(8,128)(2,1)}, bf16[192,512]{1,0:T(8,128)(2,1)}, u32[]{:S(2)}, u32[]{:S(2)}) collective-permute-start(bf16[192,512]{1,0:T(8,128)(2,1)} %get-tuple-element.87), channel_id=1, source_target_pairs={{0,3},{1,2},{2,1},{3,0},{4,7},{5,6},{6,5},{7,4},{8,11},{9,10},{10,... | collective-permute-start | bytes 589832 | tf_op jit(solution)/shard_map/ppermute | solution.py:392
  261.8 135.4 %collective-permute-start.19 = (bf16[768,768]{1,0:T(8,128)(2,1)}, bf16[768,768]{1,0:T(8,128)(2,1)S(1)}, u32[]{:S(2)}, u32[]{:S(2)}) collective-permute-start(bf16[768,768]{1,0:T(8,128)(2,1)} %convolution_convert_fusion.8), channel_id=1, source_target_pairs={{0,1},{1,0},{2,3},{3,2},{4,5},{5,4},{6,7},{7,6},{8,9},{9,8},{10,11... | collective-permute-start | bytes 3538952 | tf_op jit(solution)/shard_map/ppermute | solution.py:392
  261.8 34.6 %collective-permute-start.15 = (bf16[768,768]{1,0:T(8,128)(2,1)}, bf16[768,768]{1,0:T(8,128)(2,1)}, u32[]{:S(2)}, u32[]{:S(2)}) collective-permute-start(bf16[768,768]{1,0:T(8,128)(2,1)} %add_convert_fusion), channel_id=1, source_target_pairs={{0,2},{1,3},{2,0},{3,1},{4,6},{5,7},{6,4},{7,5},{8,10},{9,11},{10,... | collective-permute-start | bytes 3538952 | tf_op jit(solution)/shard_map/ppermute | solution.py:392
  262.1 54.1 %collective-permute-start.13 = (bf16[768,768]{1,0:T(8,128)(2,1)}, bf16[768,768]{1,0:T(8,128)(2,1)}, u32[]{:S(2)}, u32[]{:S(2)}) collective-permute-start(bf16[768,768]{1,0:T(8,128)(2,1)} %add_convert_fusion.1), channel_id=1, source_target_pairs={{0,2},{1,3},{2,0},{3,1},{4,6},{5,7},{6,4},{7,5},{8,10},{9,11},{10,... | collective-permute-start | bytes 3538952 | tf_op jit(solution)/shard_map/ppermute | solution.py:392
  267.8 54.2 %collective-permute-start.17 = (bf16[192,768]{1,0:T(8,128)(2,1)}, bf16[192,768]{1,0:T(8,128)(2,1)S(1)}, u32[]{:S(2)}, u32[]{:S(2)}) collective-permute-start(bf16[192,768]{1,0:T(8,128)(2,1)} %fusion.56), channel_id=1, source_target_pairs={{0,2},{1,3},{2,0},{3,1},{4,6},{5,7},{6,4},{7,5},{8,10},{9,11},{10,... | collective-permute-start | bytes 884744 | tf_op jit(solution)/shard_map/ppermute | solution.py:392
  268.1 53.9 %copy-start.34 = (bf16[768,192]{0,1:T(8,128)(2,1)S(1)}, bf16[768,192]{0,1:T(8,128)(2,1)}, u32[]{:S(2)}) copy-start(bf16[768,192]{0,1:T(8,128)(2,1)} %param.22) | copy-start | bytes 884740
  268.1 53.9 %copy-start.36 = (bf16[768,192]{0,1:T(8,128)(2,1)S(1)}, bf16[768,192]{0,1:T(8,128)(2,1)}, u32[]{:S(2)}) copy-start(bf16[768,192]{0,1:T(8,128)(2,1)} %param.23) | copy-start | bytes 884740
  296.3 38.1 %collective-permute-start.18 = (bf16[192,768]{1,0:T(8,128)(2,1)}, bf16[192,768]{1,0:T(8,128)(2,1)}, u32[]{:S(2)}, u32[]{:S(2)}) collective-permute-start(bf16[192,768]{1,0:T(8,128)(2,1)} %get-tuple-element.74), channel_id=1, source_target_pairs={{0,1},{1,0},{2,3},{3,2},{4,5},{5,4},{6,7},{7,6},{8,9},{9,8},{10,11... | collective-permute-start | bytes 884744 | tf_op jit(solution)/shard_map/ppermute | solution.py:392
  322.0 5.7 %copy-start.46 = (f32[768,8]{0,1:T(8,128)S(1)}, f32[768,8]{0,1:T(8,128)}, u32[]{:S(2)}) copy-start(f32[768,8]{0,1:T(8,128)} %fusion.83) | copy-start | bytes 73732
  328.4 6.0 %copy-start.45 = (bf16[192,768]{1,0:T(8,128)(2,1)S(1)}, bf16[192,768]{1,0:T(8,128)(2,1)}, u32[]{:S(2)}) copy-start(bf16[192,768]{1,0:T(8,128)(2,1)} %copy-done.44) | copy-start | bytes 884740
  336.9 48.7 %copy-start.49 = (f32[512]{0:T(512)S(1)}, f32[512]{0:T(512)}, u32[]{:S(2)}) copy-start(f32[512]{0:T(512)} %copy-done.48) | copy-start | bytes 6148
  336.9 48.7 %copy-start.50 = (f32[512]{0:T(512)S(1)}, f32[512]{0:T(512)}, u32[]{:S(2)}) copy-start(f32[512]{0:T(512)} %add_rsqrt_fusion) | copy-start | bytes 6148
  (40 other events, 119.2 us)
